TPU v7x, 1024 devices: a whole 8x8x8 slice. The times are simulated.
1024 devices in a mesh: gx: 32 (over y, z_hi, core), gy: 4 (over z_lo), gz: 8 (over x).
Axes of the slice: x: 8, y: 8, z: 8 (z_hi: 2, z_lo: 4; z = z_hi * 4 + z_lo), core: 2. Of those that a mesh axis runs over, the one named last changes fastest.
Arguments:
- les_state: float32 [5, 256, 32, 1024], P(None, 'gx', 'gy', 'gz'), may hold values from -0.4 to 0.4
- acoustic_state: float32 [4, 256, 32, 1024], P(None, 'gx', 'gy', 'gz'), may hold values from -0.04 to 0.04
- mean_flow: float32 [3, 256, 32, 1024], P(None, 'gx', 'gy', 'gz'), may hold values from -0.5 to 0.5
- projection: float32 [8, 8], replicated, may hold values from -0.3 to 1.3, as said below
- target_owner: int32 [32, 4, 128], P('gx', 'gy', 'gz'), may hold values from 0 to 31, as said below
- target_slot: int32 [32, 4, 128], P('gx', 'gy', 'gz'), may hold values from 0 to 15
Outputs:
- les_next: float32 [5, 256, 32, 1024], P(None, 'gx', 'gy', 'gz')
- source_nodes: float32 [3, 256, 32, 1024], P(None, 'gx', 'gy', 'gz')
- acoustic_next: float32 [4, 256, 32, 1024], P(None, 'gx', 'gy', 'gz')
Inputs may be any that keep to these rules, and one draw needn't show every extreme that they name: `target_owner`: the blocks of the device with index i along gx name as owners exactly the 4 consecutive indices from (i * (32 - 3)) // 32 on, each for exactly 4 blocks. `projection`: diagonal entries lie in 0.7 to 1.3, the others in -0.3 to 0.3.
All inputs are finite; a program needn't handle non-finite values.
Results may differ from a plain program's by a relative error of at most 0.00011.
Values sent between devices are 32-bit elements; how exact they have to be, the bound alone decides.
A program may use at most 32 MiB of HBM per device.

v0:
```python
import jax
import jax.numpy as jnp
import numpy as np
from jax import lax
from jax.sharding import PartitionSpec as P

EX = 1
EY = 1
EZ = 16


lobatto_points = np.array(
    [
        -1.0,
        -0.8717401485096066,
        -0.5917001814331423,
        -0.2092992179024789,
        0.2092992179024789,
        0.5917001814331423,
        0.8717401485096066,
        1.0,
    ]
)
flux_half = 0.08
viscous_ratio = 0.08
gamma_less = 0.4
acoustic_step = 0.01
upwind_speed = 1.5
face_lift = 28.0


def padded_2(cells, sides, width):
    for axis, dim in sides:
        count = lax.axis_size(axis)
        ends = count - 1
        head = lax.slice_in_dim(cells, 0, width, axis=dim)
        tail = lax.slice_in_dim(cells, cells.shape[dim] - width, cells.shape[dim], axis=dim)
        cells = jnp.concatenate(
            [
                lax.ppermute(tail, axis, [(i, (i + 1) % count) for i in range(ends)]),
                cells,
                lax.ppermute(head, axis, [((i + 1) % count, i) for i in range(ends)]),
            ],
            axis=dim,
        )
    return cells


def from_behind(block, axis, distance):
    devices = range(lax.axis_size(axis))
    route = [(i - distance, i) for i in devices if i - distance in devices]
    return lax.ppermute(block, axis, route)


def derivative_matrix():
    products = np.array(
        [
            np.prod(
                [
                    lobatto_points[row_index] - lobatto_points[partner_index]
                    for partner_index in range(8)
                    if partner_index != row_index
                ]
            )
            for row_index in range(8)
        ]
    )
    matrix = np.zeros((8, 8))
    for row_index in range(8):
        for col_index in range(8):
            if col_index != row_index:
                matrix[row_index, col_index] = products[row_index] / (
                    products[col_index] * (lobatto_points[row_index] - lobatto_points[col_index])
                )
        matrix[row_index, row_index] = -np.sum(matrix[row_index])
    return matrix


def inner_slice(padded, axis_dim, offset):
    selector = [slice(None)]
    for dim_index in range(3):
        extent = padded.shape[dim_index + 1]
        if dim_index == axis_dim:
            selector.append(slice(1 + offset, extent - 1 + offset))
        else:
            selector.append(slice(1, extent - 1))
    return padded[tuple(selector)]


def full_state(padded):
    free_stream = jnp.array([1.0, 0.0, 0.0, 0.0, 2.5], jnp.float32)[:, None, None, None]
    return padded + free_stream


def les_rate(padded):
    state_full = full_state(padded)
    density = state_full[0]
    momentum = state_full[1:4]
    energy = state_full[4]
    velocity = momentum / density
    pressure = gamma_less * (energy - 0.5 * jnp.sum(momentum * velocity, axis=0))
    center = inner_slice(padded, 0, 0)
    change = jnp.zeros_like(center)
    for axis_dim in range(3):
        axis_speed = velocity[axis_dim]
        flux_rows = [momentum[axis_dim]]
        for component in range(3):
            term = momentum[component] * axis_speed
            if component == axis_dim:
                term = term + pressure
            flux_rows.append(term)
        flux_rows.append((energy + pressure) * axis_speed)
        fluxes = jnp.stack(flux_rows)
        change = change - flux_half * (
            inner_slice(fluxes, axis_dim, 1) - inner_slice(fluxes, axis_dim, -1)
        )
        change = change + viscous_ratio * (
            inner_slice(padded, axis_dim, 1) + inner_slice(padded, axis_dim, -1) - 2.0 * center
        )
    return change


def lamb_vector(padded):
    state_full = full_state(padded)
    velocity = state_full[1:4] / state_full[0]

    def slope(component, axis_dim):
        return 0.5 * (
            inner_slice(velocity, axis_dim, 1)[component]
            - inner_slice(velocity, axis_dim, -1)[component]
        )

    vort_x = slope(2, 1) - slope(1, 2)
    vort_y = slope(0, 2) - slope(2, 0)
    vort_z = slope(1, 0) - slope(0, 1)
    speed = inner_slice(velocity, 0, 0)
    return jnp.stack(
        [
            vort_y * speed[2] - vort_z * speed[1],
            vort_z * speed[0] - vort_x * speed[2],
            vort_x * speed[1] - vort_y * speed[0],
        ]
    )


def project_blocks(lamb_field, projection):
    component_count, size_x, size_y, size_z = lamb_field.shape
    blocks = lamb_field.reshape(
        component_count, size_x // 8, 8, size_y // 8, 8, size_z // 8, 8
    ).transpose(1, 3, 5, 0, 2, 4, 6)
    highest = lax.Precision.HIGHEST
    blocks = jnp.einsum("ia,xyzcabe->xyzcibe", projection, blocks, precision=highest)
    blocks = jnp.einsum("jb,xyzcibe->xyzcije", projection, blocks, precision=highest)
    blocks = jnp.einsum("ke,xyzcije->xyzcijk", projection, blocks, precision=highest)
    return blocks.reshape(-1, component_count * 512)


def flux_along(state_now, mean_speed, axis_dim):
    pressure = state_now[0]
    axis_speed = mean_speed[axis_dim]
    flux_rows = [axis_speed * pressure + state_now[1 + axis_dim]]
    for component in range(3):
        term = axis_speed * state_now[1 + component]
        if component == axis_dim:
            term = term + pressure
        flux_rows.append(term)
    return jnp.stack(flux_rows)


def element_derivative(field_data, axis_dim):
    extent = field_data.shape[axis_dim + 1]
    deriv_table = jnp.asarray(np.kron(np.eye(extent // 8), derivative_matrix()), jnp.float32)
    highest = lax.Precision.HIGHEST
    if axis_dim == 0:
        return jnp.einsum("ckyz,jk->cjyz", field_data, deriv_table, precision=highest)
    if axis_dim == 1:
        return jnp.einsum("cxkz,jk->cxjz", field_data, deriv_table, precision=highest)
    return jnp.einsum("cxyk,jk->cxyj", field_data, deriv_table, precision=highest)


def acoustic_rate(padded, mean_speed, source):
    center = inner_slice(padded, 0, 0)
    total_rate = jnp.zeros_like(center)
    for axis_dim in range(3):
        extent = center.shape[axis_dim + 1]
        position = jnp.arange(extent) % 8
        shape_list = [1, 1, 1, 1]
        shape_list[axis_dim + 1] = extent
        right_face = (position == 7).astype(jnp.float32).reshape(shape_list)
        left_face = (position == 0).astype(jnp.float32).reshape(shape_list)
        upper_jump = inner_slice(padded, axis_dim, 1) - center
        lower_jump = inner_slice(padded, axis_dim, -1) - center
        total_rate = total_rate - element_derivative(
            flux_along(center, mean_speed, axis_dim), axis_dim
        )
        total_rate = total_rate - right_face * face_lift * (
            0.5 * flux_along(upper_jump, mean_speed, axis_dim) - 0.5 * upwind_speed * upper_jump
        )
        total_rate = total_rate + left_face * face_lift * (
            0.5 * flux_along(lower_jump, mean_speed, axis_dim) + 0.5 * upwind_speed * lower_jump
        )
    return total_rate + jnp.concatenate([jnp.zeros_like(source[:1]), source], axis=0)


def les_halo(field_data):
    return padded_2(field_data, (("gx", 1), ("gy", 2), ("gz", 3)), 1)


def trace_halo(field_data):
    return padded_2(field_data, (("gx", 1), ("gy", 2), ("gz", 3)), 1)


def pack_blocks(coeffs, key_index, slot_ids, key_count, capacity):
    onehot = (key_index[:, None] == jnp.arange(key_count, dtype=jnp.int32)[None, :]).astype(
        jnp.int32
    )
    before = jnp.cumsum(onehot, axis=0) - onehot
    position = jnp.sum(before * onehot, axis=1)
    flat_index = key_index * capacity + position
    placement_matrix = (
        flat_index[:, None] == jnp.arange(key_count * capacity, dtype=jnp.int32)[None, :]
    )
    buffer = jnp.einsum(
        "ns,nf->sf", placement_matrix.astype(jnp.float32), coeffs, precision=lax.Precision.HIGHEST
    )
    labels = jnp.sum(placement_matrix.astype(jnp.int32) * (slot_ids[:, None] + 1), axis=0) - 1
    return (buffer, labels)


def accumulate(piece_data, piece_labels, element_count):
    onehot = (jnp.arange(element_count, dtype=jnp.int32)[:, None] == piece_labels[None, :]).astype(
        jnp.float32
    )
    return jnp.dot(onehot, piece_data, precision=lax.Precision.HIGHEST)


def local(les_state, acoustic_state, mean_flow, projection, target_owner, target_slot):
    acoustic_padded = None
    section_state = None
    second_rate = None
    first_padded = les_halo(les_state)
    first_rate = les_rate(first_padded)
    section_state = les_state + first_rate
    lamb_field = lamb_vector(first_padded)
    coeffs = project_blocks(lamb_field, projection)
    owners = target_owner.reshape(-1)
    slot_ids = target_slot.reshape(-1)
    block_count = owners.shape[0]
    owner_count = lax.axis_size("gx")
    window = min(4, owner_count)
    capacity = block_count // window
    element_count = EX * EY * EZ
    own_index = lax.axis_index("gx")
    key_count = 2 * window - 1
    buffer, labels = pack_blocks(
        coeffs, owners - own_index + (window - 1), slot_ids, key_count, capacity
    )
    buffer = buffer.reshape(key_count, capacity, buffer.shape[-1])
    labels = labels.reshape(key_count, capacity)
    element_sums = accumulate(buffer[window - 1], labels[window - 1], element_count)
    for offset in range(1 - window, window):
        if offset != 0:
            piece_data, piece_labels = from_behind(
                (buffer[offset + window - 1], labels[offset + window - 1]), "gx", offset
            )
            element_sums = element_sums + accumulate(piece_data, piece_labels, element_count)
    source_nodes = (
        element_sums.reshape(EX, EY, EZ, 3, 8, 8, 8)
        .transpose(3, 0, 4, 1, 5, 2, 6)
        .reshape(3, EX * 8, EY * 8, EZ * 8)
    )
    acoustic_padded = trace_halo(acoustic_state)
    first_acoustic = acoustic_rate(acoustic_padded, mean_flow, source_nodes)
    middle_state = acoustic_state + acoustic_step * first_acoustic
    second_rate = les_rate(les_halo(section_state))
    middle_padded = trace_halo(middle_state)
    les_next = les_state + 0.5 * (first_rate + second_rate)
    second_acoustic = acoustic_rate(middle_padded, mean_flow, source_nodes)
    acoustic_next = acoustic_state + 0.5 * acoustic_step * (first_acoustic + second_acoustic)
    return (les_next, source_nodes, acoustic_next)


def solution(mesh):
    return jax.shard_map(
        local,
        mesh=mesh,
        in_specs=(
            P(None, "gx", "gy", "gz"),
            P(None, "gx", "gy", "gz"),
            P(None, "gx", "gy", "gz"),
            P(),
            P("gx", "gy", "gz"),
            P("gx", "gy", "gz"),
        ),
        out_specs=(P(None, "gx", "gy", "gz"), P(None, "gx", "gy", "gz"), P(None, "gx", "gy", "gz")),
        check_vma=False,
    )
```

profile of v0, /device:TPU:70, one launch (start us, length us, event | category | flops | bytes accessed | tf_op | source)
XLA Modules:
  0.0 233.8 jit_solution(4461001074273953396)
XLA Ops:
  3.7 14.3 %collective-permute-start.14 = (s32[4]{0:T(128)}, s32[4]{0:T(128)}, u32[]{:S(2)}, u32[]{:S(2)}) collective-permute-start(s32[4]{0:T(128)} %get-tuple-element.210), channel_id=1, source_target_pairs={{64,0},{96,32},{128,64},{160,96},{192,128},{224,160},{256,192},{28... | collective-permute-start | bytes 56 | tf_op jit(solution)/shard_map/ppermute | solution.py:52
  18.1 1.9 collective-permute-start.22
  20.0 8.1 %collective-permute-start.20 = (s32[4]{0:T(128)}, s32[4]{0:T(128)}, u32[]{:S(2)}, u32[]{:S(2)}) collective-permute-start(s32[4]{0:T(128)} %get-tuple-element.212), channel_id=1, source_target_pairs={{0,64},{32,96},{64,128},{96,160},{128,192},{160,224},{192,256},{22... | collective-permute-start | bytes 56 | tf_op jit(solution)/shard_map/ppermute | solution.py:52
  28.9 4.8 %collective-permute-start.24 = (f32[4,1,8,128]{3,1,2,0:T(1,128)S(1)}, f32[4,1,8,128]{3,1,2,0:T(1,128)S(1)}, u32[]{:S(2)}, u32[]{:S(2)}) collective-permute-start(f32[4,1,8,128]{3,1,2,0:T(1,128)S(1)} %bitcast.112), channel_id=1, source_target_pairs={{32,0},{64,32},{96,64},{128,96},{160,128},{192,160},{224,192},{256... | collective-permute-start | bytes 49160 | tf_op jit(solution)/shard_map/ppermute | solution.py:42
  33.7 1.9 collective-permute-start.25
  40.4 9.6 %collective-permute-start.1 = (f32[5,1,8,128]{3,2,1,0:T(8,128)S(1)}, f32[5,1,8,128]{3,2,1,0:T(8,128)S(1)}, u32[]{:S(2)}, u32[]{:S(2)}) collective-permute-start(f32[5,1,8,128]{3,2,1,0:T(8,128)S(1)} %get-tuple-element.155), channel_id=1, source_target_pairs={{32,0},{64,32},{96,64},{128,96},{160,128},{192,160},{224,192},{256... | collective-permute-start | bytes 61448 | tf_op jit(solution)/shard_map/ppermute | solution.py:42
  50.1 1.9 collective-permute-start
  52.0 9.3 %collective-permute-done = f32[5,1,8,128]{3,2,1,0:T(8,128)S(1)} collective-permute-done((f32[5,1,8,128]{3,2,1,0:T(8,128)S(1)}, f32[5,1,8,128]{3,2,1,0:T(8,128)S(1)}, u32[]{:S(2)}, u32[]{:S(2)}) %collective-permute-start) | collective-permute-done | bytes 20512 | tf_op jit(solution)/shard_map/ppermute | solution.py:40
  61.3 4.2 %collective-permute-start.27 = (f32[4,10,1,128]{3,1,2,0:T(8,128)S(1)}, f32[4,10,1,128]{3,1,2,0:T(8,128)S(1)}, u32[]{:S(2)}, u32[]{:S(2)}) collective-permute-start(f32[4,10,1,128]{3,1,2,0:T(8,128)S(1)} %get-tuple-element.135), channel_id=1, source_target_pairs={{0,8},{8,16},{16,24},{1,9},{9,17},{17,25},{2,10},{10,18},{18,26},{... | collective-permute-start | bytes 61448 | tf_op jit(solution)/shard_map/ppermute | solution.py:40
  67.0 4.8 %collective-permute-done.26 = f32[4,10,1,128]{3,1,2,0:T(8,128)S(1)} collective-permute-done((f32[4,10,1,128]{3,1,2,0:T(8,128)S(1)}, f32[4,10,1,128]{3,1,2,0:T(8,128)S(1)}, u32[]{:S(2)}, u32[]{:S(2)}) %collective-permute-start.26) | collective-permute-done | bytes 20512 | tf_op jit(solution)/shard_map/ppermute | solution.py:42
  72.0 4.6 %collective-permute-start.29 = (f32[4,10,10,1]{3,1,2,0:T(8,128)S(1)}, f32[4,10,10,1]{3,1,2,0:T(8,128)S(1)}, u32[]{:S(2)}, u32[]{:S(2)}) collective-permute-start(f32[4,10,10,1]{3,1,2,0:T(8,128)S(1)} %get-tuple-element.59), channel_id=1, source_target_pairs={{0,1},{1,2},{2,3},{3,4},{4,5},{5,6},{6,7},{8,9},{9,10},{10,11},{11... | collective-permute-start | bytes 4808 | tf_op jit(solution)/shard_map/ppermute | solution.py:40
  76.7 1.9 collective-permute-start.28
  78.7 2.6 %collective-permute-done.29 = f32[4,10,10,1]{3,1,2,0:T(8,128)S(1)} collective-permute-done((f32[4,10,10,1]{3,1,2,0:T(8,128)S(1)}, f32[4,10,10,1]{3,1,2,0:T(8,128)S(1)}, u32[]{:S(2)}, u32[]{:S(2)}) %collective-permute-start.29) | collective-permute-done | bytes 1632 | tf_op jit(solution)/shard_map/ppermute | solution.py:40
  81.2 4.2 %collective-permute-start.2 = (f32[5,10,1,128]{3,2,1,0:T(1,128)S(1)}, f32[5,10,1,128]{3,2,1,0:T(1,128)S(1)}, u32[]{:S(2)}, u32[]{:S(2)}) collective-permute-start(f32[5,10,1,128]{3,2,1,0:T(1,128)S(1)} %get-tuple-element.67), channel_id=1, source_target_pairs={{0,8},{8,16},{16,24},{1,9},{9,17},{17,25},{2,10},{10,18},{18,26},{... | collective-permute-start | bytes 76808 | tf_op jit(solution)/shard_map/ppermute | solution.py:40
  85.4 1.4 collective-permute-done.28
  89.5 3.3 %collective-permute-done.3 = f32[5,10,1,128]{3,2,1,0:T(1,128)S(1)} collective-permute-done((f32[5,10,1,128]{3,2,1,0:T(1,128)S(1)}, f32[5,10,1,128]{3,2,1,0:T(1,128)S(1)}, u32[]{:S(2)}, u32[]{:S(2)}) %collective-permute-start.3) | collective-permute-done | bytes 25632 | tf_op jit(solution)/shard_map/ppermute | solution.py:42
  93.1 1.9 collective-permute-start.5
  95.0 5.1 %collective-permute-start.4 = (f32[5,10,10,1]{3,2,1,0:T(8,128)S(1)}, f32[5,10,10,1]{3,2,1,0:T(8,128)S(1)}, u32[]{:S(2)}, u32[]{:S(2)}) collective-permute-start(f32[5,10,10,1]{3,2,1,0:T(8,128)S(1)} %get-tuple-element.56), channel_id=1, source_target_pairs={{0,1},{1,2},{2,3},{3,4},{4,5},{5,6},{6,7},{8,9},{9,10},{10,11},{11... | collective-permute-start | bytes 6008 | tf_op jit(solution)/shard_map/ppermute | solution.py:40
  100.9 3.3 %collective-permute-done.5 = f32[5,10,10,1]{3,2,1,0:T(8,128)S(1)} collective-permute-done((f32[5,10,10,1]{3,2,1,0:T(8,128)S(1)}, f32[5,10,10,1]{3,2,1,0:T(8,128)S(1)}, u32[]{:S(2)}, u32[]{:S(2)}) %collective-permute-start.5) | collective-permute-done | bytes 2032 | tf_op jit(solution)/shard_map/ppermute | solution.py:42
  104.2 1.5 collective-permute-done.4
  111.7 1.9 convolution_bitcast_fusion.1
  118.6 1.9 collective-permute-start.6
  120.5 9.7 %collective-permute-start.7 = (f32[5,1,8,128]{3,2,1,0:T(8,128)S(1)}, f32[5,1,8,128]{3,2,1,0:T(8,128)S(1)}, u32[]{:S(2)}, u32[]{:S(2)}) collective-permute-start(f32[5,1,8,128]{3,2,1,0:T(8,128)S(1)} %get-tuple-element.154), channel_id=1, source_target_pairs={{32,0},{64,32},{96,64},{128,96},{160,128},{192,160},{224,192},{256... | collective-permute-start | bytes 61448 | tf_op jit(solution)/shard_map/ppermute | solution.py:42
  130.3 1.9 collective-permute-start.12
  132.3 1.9 collective-permute-start.13
  134.9 4.3 %collective-permute-done.12 = s32[4]{0:T(128)S(1)} collective-permute-done((s32[4]{0:T(128)S(1)}, s32[4]{0:T(128)S(1)}, u32[]{:S(2)}, u32[]{:S(2)}) %collective-permute-start.12) | collective-permute-done | bytes 48 | tf_op jit(solution)/shard_map/ppermute | solution.py:52
  139.1 4.8 %collective-permute-start.16 = (s32[4]{0:T(128)S(1)}, s32[4]{0:T(128)S(1)}, u32[]{:S(2)}, u32[]{:S(2)}) collective-permute-start(s32[4]{0:T(128)S(1)} %copy-done.38), channel_id=1, source_target_pairs={{32,0},{64,32},{96,64},{128,96},{160,128},{192,160},{224,192},{256... | collective-permute-start | bytes 56 | tf_op jit(solution)/shard_map/ppermute | solution.py:52
  144.0 3.7 %collective-permute-start.17 = (f32[4,1536]{1,0:T(4,128)S(1)}, f32[4,1536]{1,0:T(4,128)S(1)}, u32[]{:S(2)}, u32[]{:S(2)}) collective-permute-start(f32[4,1536]{1,0:T(4,128)S(1)} %get-tuple-element.75), channel_id=1, source_target_pairs={{32,0},{64,32},{96,64},{128,96},{160,128},{192,160},{224,192},{256... | collective-permute-start | bytes 73736 | tf_op jit(solution)/shard_map/ppermute | solution.py:52
  147.9 1.9 collective-permute-start.18
  149.8 3.3 %collective-permute-start.19 = (f32[4,1536]{1,0:T(4,128)S(1)}, f32[4,1536]{1,0:T(4,128)S(1)}, u32[]{:S(2)}, u32[]{:S(2)}) collective-permute-start(f32[4,1536]{1,0:T(4,128)S(1)} %get-tuple-element.74), channel_id=1, source_target_pairs={{0,32},{32,64},{64,96},{96,128},{128,160},{160,192},{192,224},{224... | collective-permute-start | bytes 73736 | tf_op jit(solution)/shard_map/ppermute | solution.py:52
  153.4 5.5 %collective-permute-done.18 = s32[4]{0:T(128)S(1)} collective-permute-done((s32[4]{0:T(128)S(1)}, s32[4]{0:T(128)S(1)}, u32[]{:S(2)}, u32[]{:S(2)}) %collective-permute-start.18) | collective-permute-done | bytes 48 | tf_op jit(solution)/shard_map/ppermute | solution.py:52
  158.8 3.2 %collective-permute-start.15 = (f32[4,1536]{1,0:T(4,128)S(1)}, f32[4,1536]{1,0:T(4,128)S(1)}, u32[]{:S(2)}, u32[]{:S(2)}) collective-permute-start(f32[4,1536]{1,0:T(4,128)S(1)} %get-tuple-element.71), channel_id=1, source_target_pairs={{64,0},{96,32},{128,64},{160,96},{192,128},{224,160},{256,192},{28... | collective-permute-start | bytes 73736 | tf_op jit(solution)/shard_map/ppermute | solution.py:52
  162.0 6.5 %collective-permute-start.21 = (f32[4,1536]{1,0:T(4,128)S(1)}, f32[4,1536]{1,0:T(4,128)S(1)}, u32[]{:S(2)}, u32[]{:S(2)}) collective-permute-start(f32[4,1536]{1,0:T(4,128)S(1)} %get-tuple-element.73), channel_id=1, source_target_pairs={{0,64},{32,96},{64,128},{96,160},{128,192},{160,224},{192,256},{22... | collective-permute-start | bytes 73736 | tf_op jit(solution)/shard_map/ppermute | solution.py:52
  168.8 1.9 collective-permute-start.23
  170.7 3.1 %collective-permute-done.21 = f32[4,1536]{1,0:T(4,128)S(1)} collective-permute-done((f32[4,1536]{1,0:T(4,128)S(1)}, f32[4,1536]{1,0:T(4,128)S(1)}, u32[]{:S(2)}, u32[]{:S(2)}) %collective-permute-start.21) | collective-permute-done | bytes 24608 | tf_op jit(solution)/shard_map/ppermute | solution.py:52
  173.8 4.7 %collective-permute-start.8 = (f32[5,10,1,128]{3,2,1,0:T(1,128)}, f32[5,10,1,128]{3,2,1,0:T(1,128)}, u32[]{:S(2)}, u32[]{:S(2)}) collective-permute-start(f32[5,10,1,128]{3,2,1,0:T(1,128)} %get-tuple-element.65), channel_id=1, source_target_pairs={{0,8},{8,16},{16,24},{1,9},{9,17},{17,25},{2,10},{10,18},{18,26},{... | collective-permute-start | bytes 76808 | tf_op jit(solution)/shard_map/ppermute | solution.py:40
  179.3 1.5 collective-permute-start.9
  184.8 1.9 collective-permute-start.31
  186.8 9.7 %collective-permute-start.30 = (f32[4,1,8,128]{3,1,2,0:T(1,128)S(1)}, f32[4,1,8,128]{3,1,2,0:T(1,128)S(1)}, u32[]{:S(2)}, u32[]{:S(2)}) collective-permute-start(f32[4,1,8,128]{3,1,2,0:T(1,128)S(1)} %get-tuple-element.168), channel_id=1, source_target_pairs={{32,0},{64,32},{96,64},{128,96},{160,128},{192,160},{224,192},{256... | collective-permute-start | bytes 49160 | tf_op jit(solution)/shard_map/ppermute | solution.py:42
  197.8 1.9 collective-permute-start.11
  199.7 5.6 %collective-permute-start.10 = (f32[5,10,10,1]{3,2,1,0:T(8,128)S(1)}, f32[5,10,10,1]{3,2,1,0:T(8,128)S(1)}, u32[]{:S(2)}, u32[]{:S(2)}) collective-permute-start(f32[5,10,10,1]{3,2,1,0:T(8,128)S(1)} %get-tuple-element.54), channel_id=1, source_target_pairs={{0,1},{1,2},{2,3},{3,4},{4,5},{5,6},{6,7},{8,9},{9,10},{10,11},{11... | collective-permute-start | bytes 6008 | tf_op jit(solution)/shard_map/ppermute | solution.py:40
  205.4 4.5 %collective-permute-start.33 = (f32[4,10,1,128]{3,1,2,0:T(8,128)S(1)}, f32[4,10,1,128]{3,1,2,0:T(8,128)S(1)}, u32[]{:S(2)}, u32[]{:S(2)}) collective-permute-start(f32[4,10,1,128]{3,1,2,0:T(8,128)S(1)} %get-tuple-element.97), channel_id=1, source_target_pairs={{0,8},{8,16},{16,24},{1,9},{9,17},{17,25},{2,10},{10,18},{18,26},{... | collective-permute-start | bytes 61448 | tf_op jit(solution)/shard_map/ppermute | solution.py:40
  211.2 1.4 maximum_add_fusion.1
  213.9 2.1 fusion.38
  216.2 5.2 %collective-permute-start.35 = (f32[4,10,10,1]{3,1,2,0:T(8,128)S(1)}, f32[4,10,10,1]{3,1,2,0:T(8,128)S(1)}, u32[]{:S(2)}, u32[]{:S(2)}) collective-permute-start(f32[4,10,10,1]{3,1,2,0:T(8,128)S(1)} %get-tuple-element.57), channel_id=1, source_target_pairs={{0,1},{1,2},{2,3},{3,4},{4,5},{5,6},{6,7},{8,9},{9,10},{10,11},{11... | collective-permute-start | bytes 4808 | tf_op jit(solution)/shard_map/ppermute | solution.py:40
  221.4 1.9 collective-permute-start.34
  223.5 2.6 %collective-permute-done.35 = f32[4,10,10,1]{3,1,2,0:T(8,128)S(1)} collective-permute-done((f32[4,10,10,1]{3,1,2,0:T(8,128)S(1)}, f32[4,10,10,1]{3,1,2,0:T(8,128)S(1)}, u32[]{:S(2)}, u32[]{:S(2)}) %collective-permute-start.35) | collective-permute-done | bytes 1632 | tf_op jit(solution)/shard_map/ppermute | solution.py:40
  226.0 5.6 %collective-permute-done.34 = f32[4,10,10,1]{3,1,2,0:T(8,128)S(1)} collective-permute-done((f32[4,10,10,1]{3,1,2,0:T(8,128)S(1)}, f32[4,10,10,1]{3,1,2,0:T(8,128)S(1)}, u32[]{:S(2)}, u32[]{:S(2)}) %collective-permute-start.34) | collective-permute-done | bytes 1632 | tf_op jit(solution)/shard_map/ppermute | solution.py:42
  (212 shorter events, 36.8 us)
Async XLA Ops:
  0.6 111.1 %copy-start = (f32[8,8]{1,0:T(8,128)S(1)}, f32[8,8]{1,0:T(8,128)}, u32[]{:S(2)}) copy-start(f32[8,8]{1,0:T(8,128)} %param.18) | copy-start | bytes 772
  0.6 64.8 %copy-start.1 = (f32[5,8,8,128]{3,2,1,0:T(8,128)S(1)}, f32[5,8,8,128]{3,2,1,0:T(8,128)}, u32[]{:S(2)}) copy-start(f32[5,8,8,128]{3,2,1,0:T(8,128)} %param.15) | copy-start | bytes 491524
  3.7 177.9 %collective-permute-start.14 = (s32[4]{0:T(128)}, s32[4]{0:T(128)}, u32[]{:S(2)}, u32[]{:S(2)}) collective-permute-start(s32[4]{0:T(128)} %get-tuple-element.210), channel_id=1, source_target_pairs={{64,0},{96,32},{128,64},{160,96},{192,128},{224,160},{256,192},{28... | collective-permute-start | bytes 56 | tf_op jit(solution)/shard_map/ppermute | solution.py:52
  18.1 161.2 %collective-permute-start.22 = (s32[4]{0:T(128)}, s32[4]{0:T(128)}, u32[]{:S(2)}, u32[]{:S(2)}) collective-permute-start(s32[4]{0:T(128)} %get-tuple-element.211), channel_id=1, source_target_pairs={{0,96},{32,128},{64,160},{96,192},{128,224},{160,256},{192,288},{2... | collective-permute-start | bytes 56 | tf_op jit(solution)/shard_map/ppermute | solution.py:52
  20.0 148.8 %collective-permute-start.20 = (s32[4]{0:T(128)}, s32[4]{0:T(128)}, u32[]{:S(2)}, u32[]{:S(2)}) collective-permute-start(s32[4]{0:T(128)} %get-tuple-element.212), channel_id=1, source_target_pairs={{0,64},{32,96},{64,128},{96,160},{128,192},{160,224},{192,256},{22... | collective-permute-start | bytes 56 | tf_op jit(solution)/shard_map/ppermute | solution.py:52
  28.9 11.5 %collective-permute-start.24 = (f32[4,1,8,128]{3,1,2,0:T(1,128)S(1)}, f32[4,1,8,128]{3,1,2,0:T(1,128)S(1)}, u32[]{:S(2)}, u32[]{:S(2)}) collective-permute-start(f32[4,1,8,128]{3,1,2,0:T(1,128)S(1)} %bitcast.112), channel_id=1, source_target_pairs={{32,0},{64,32},{96,64},{128,96},{160,128},{192,160},{224,192},{256... | collective-permute-start | bytes 49160 | tf_op jit(solution)/shard_map/ppermute | solution.py:42
  33.7 16.3 %collective-permute-start.25 = (f32[4,1,8,128]{3,1,2,0:T(1,128)S(1)}, f32[4,1,8,128]{3,1,2,0:T(1,128)S(1)}, u32[]{:S(2)}, u32[]{:S(2)}) collective-permute-start(f32[4,1,8,128]{3,1,2,0:T(1,128)S(1)} %bitcast.111), channel_id=1, source_target_pairs={{0,32},{32,64},{64,96},{96,128},{128,160},{160,192},{192,224},{224... | collective-permute-start | bytes 49160 | tf_op jit(solution)/shard_map/ppermute | solution.py:40
  35.7 52.8 %copy-start.40 = (f32[8]{0:T(128)}, f32[8]{0:T(128)S(1)}, u32[]{:S(2)}) copy-start(f32[8]{0:T(128)S(1)} %get-tuple-element.219) | copy-start | bytes 100
  35.7 52.8 %copy-start.42 = (f32[8]{0:T(128)}, f32[8]{0:T(128)S(1)}, u32[]{:S(2)}) copy-start(f32[8]{0:T(128)S(1)} %get-tuple-element.220) | copy-start | bytes 100
  38.2 50.3 %copy-start.8 = (f32[1,8,8,128]{3,2,1,0:T(8,128)}, f32[1,8,8,128]{3,2,1,0:T(8,128)S(1)}, u32[]{:S(2)}) copy-start(f32[1,8,8,128]{3,2,1,0:T(8,128)S(1)} %get-tuple-element.177) | copy-start | bytes 98308
  40.4 25.1 %collective-permute-start.1 = (f32[5,1,8,128]{3,2,1,0:T(8,128)S(1)}, f32[5,1,8,128]{3,2,1,0:T(8,128)S(1)}, u32[]{:S(2)}, u32[]{:S(2)}) collective-permute-start(f32[5,1,8,128]{3,2,1,0:T(8,128)S(1)} %get-tuple-element.155), channel_id=1, source_target_pairs={{32,0},{64,32},{96,64},{128,96},{160,128},{192,160},{224,192},{256... | collective-permute-start | bytes 61448 | tf_op jit(solution)/shard_map/ppermute | solution.py:42
  50.1 11.2 %collective-permute-start = (f32[5,1,8,128]{3,2,1,0:T(8,128)S(1)}, f32[5,1,8,128]{3,2,1,0:T(8,128)S(1)}, u32[]{:S(2)}, u32[]{:S(2)}) collective-permute-start(f32[5,1,8,128]{3,2,1,0:T(8,128)S(1)} %get-tuple-element.156), channel_id=1, source_target_pairs={{0,32},{32,64},{64,96},{96,128},{128,160},{160,192},{192,224},{224... | collective-permute-start | bytes 61448 | tf_op jit(solution)/shard_map/ppermute | solution.py:40
  61.3 5.8 %collective-permute-start.27 = (f32[4,10,1,128]{3,1,2,0:T(8,128)S(1)}, f32[4,10,1,128]{3,1,2,0:T(8,128)S(1)}, u32[]{:S(2)}, u32[]{:S(2)}) collective-permute-start(f32[4,10,1,128]{3,1,2,0:T(8,128)S(1)} %get-tuple-element.135), channel_id=1, source_target_pairs={{0,8},{8,16},{16,24},{1,9},{9,17},{17,25},{2,10},{10,18},{18,26},{... | collective-permute-start | bytes 61448 | tf_op jit(solution)/shard_map/ppermute | solution.py:40
  65.5 6.3 %collective-permute-start.26 = (f32[4,10,1,128]{3,1,2,0:T(8,128)S(1)}, f32[4,10,1,128]{3,1,2,0:T(8,128)S(1)}, u32[]{:S(2)}, u32[]{:S(2)}) collective-permute-start(f32[4,10,1,128]{3,1,2,0:T(8,128)S(1)} %get-tuple-element.136), channel_id=1, source_target_pairs={{8,0},{16,8},{24,16},{9,1},{17,9},{25,17},{10,2},{18,10},{26,18},{... | collective-permute-start | bytes 61448 | tf_op jit(solution)/shard_map/ppermute | solution.py:42
  72.0 9.2 %collective-permute-start.29 = (f32[4,10,10,1]{3,1,2,0:T(8,128)S(1)}, f32[4,10,10,1]{3,1,2,0:T(8,128)S(1)}, u32[]{:S(2)}, u32[]{:S(2)}) collective-permute-start(f32[4,10,10,1]{3,1,2,0:T(8,128)S(1)} %get-tuple-element.59), channel_id=1, source_target_pairs={{0,1},{1,2},{2,3},{3,4},{4,5},{5,6},{6,7},{8,9},{9,10},{10,11},{11... | collective-permute-start | bytes 4808 | tf_op jit(solution)/shard_map/ppermute | solution.py:40
  76.7 10.2 %collective-permute-start.28 = (f32[4,10,10,1]{3,1,2,0:T(8,128)S(1)}, f32[4,10,10,1]{3,1,2,0:T(8,128)S(1)}, u32[]{:S(2)}, u32[]{:S(2)}) collective-permute-start(f32[4,10,10,1]{3,1,2,0:T(8,128)S(1)} %get-tuple-element.60), channel_id=1, source_target_pairs={{1,0},{2,1},{3,2},{4,3},{5,4},{6,5},{7,6},{9,8},{10,9},{11,10},{12... | collective-permute-start | bytes 4808 | tf_op jit(solution)/shard_map/ppermute | solution.py:42
  81.2 8.3 %collective-permute-start.2 = (f32[5,10,1,128]{3,2,1,0:T(1,128)S(1)}, f32[5,10,1,128]{3,2,1,0:T(1,128)S(1)}, u32[]{:S(2)}, u32[]{:S(2)}) collective-permute-start(f32[5,10,1,128]{3,2,1,0:T(1,128)S(1)} %get-tuple-element.67), channel_id=1, source_target_pairs={{0,8},{8,16},{16,24},{1,9},{9,17},{17,25},{2,10},{10,18},{18,26},{... | collective-permute-start | bytes 76808 | tf_op jit(solution)/shard_map/ppermute | solution.py:40
  86.9 6.0 %collective-permute-start.3 = (f32[5,10,1,128]{3,2,1,0:T(1,128)S(1)}, f32[5,10,1,128]{3,2,1,0:T(1,128)S(1)}, u32[]{:S(2)}, u32[]{:S(2)}) collective-permute-start(f32[5,10,1,128]{3,2,1,0:T(1,128)S(1)} %get-tuple-element.68), channel_id=1, source_target_pairs={{8,0},{16,8},{24,16},{9,1},{17,9},{25,17},{10,2},{18,10},{26,18},{... | collective-permute-start | bytes 76808 | tf_op jit(solution)/shard_map/ppermute | solution.py:42
  89.5 16.1 %copy-start.34 = (f32[5]{0:T(128)S(1)}, f32[5]{0:T(128)}, u32[]{:S(2)}) copy-start(f32[5]{0:T(128)} %constant.102.clone) | copy-start | bytes 64
  93.1 11.1 %collective-permute-start.5 = (f32[5,10,10,1]{3,2,1,0:T(8,128)S(1)}, f32[5,10,10,1]{3,2,1,0:T(8,128)S(1)}, u32[]{:S(2)}, u32[]{:S(2)}) collective-permute-start(f32[5,10,10,1]{3,2,1,0:T(8,128)S(1)} %get-tuple-element.55), channel_id=1, source_target_pairs={{1,0},{2,1},{3,2},{4,3},{5,4},{6,5},{7,6},{9,8},{10,9},{11,10},{12... | collective-permute-start | bytes 6008 | tf_op jit(solution)/shard_map/ppermute | solution.py:42
  95.0 10.6 %collective-permute-start.4 = (f32[5,10,10,1]{3,2,1,0:T(8,128)S(1)}, f32[5,10,10,1]{3,2,1,0:T(8,128)S(1)}, u32[]{:S(2)}, u32[]{:S(2)}) collective-permute-start(f32[5,10,10,1]{3,2,1,0:T(8,128)S(1)} %get-tuple-element.56), channel_id=1, source_target_pairs={{0,1},{1,2},{2,3},{3,4},{4,5},{5,6},{6,7},{8,9},{9,10},{10,11},{11... | collective-permute-start | bytes 6008 | tf_op jit(solution)/shard_map/ppermute | solution.py:40
  116.8 13.5 %copy-start.39 = (s32[4]{0:T(128)S(1)}, s32[4]{0:T(128)}, u32[]{:S(2)}) copy-start(s32[4]{0:T(128)} %get-tuple-element.215) | copy-start | bytes 52
  116.8 22.3 %copy-start.38 = (s32[4]{0:T(128)S(1)}, s32[4]{0:T(128)}, u32[]{:S(2)}) copy-start(s32[4]{0:T(128)} %get-tuple-element.214) | copy-start | bytes 52
  117.3 30.6 %copy-start.37 = (s32[4]{0:T(128)S(1)}, s32[4]{0:T(128)}, u32[]{:S(2)}) copy-start(s32[4]{0:T(128)} %get-tuple-element.213) | copy-start | bytes 52
  118.6 11.8 %collective-permute-start.6 = (f32[5,1,8,128]{3,2,1,0:T(8,128)S(1)}, f32[5,1,8,128]{3,2,1,0:T(8,128)S(1)}, u32[]{:S(2)}, u32[]{:S(2)}) collective-permute-start(f32[5,1,8,128]{3,2,1,0:T(8,128)S(1)} %get-tuple-element.153), channel_id=1, source_target_pairs={{0,32},{32,64},{64,96},{96,128},{128,160},{160,192},{192,224},{224... | collective-permute-start | bytes 61448 | tf_op jit(solution)/shard_map/ppermute | solution.py:40
  120.5 11.8 %collective-permute-start.7 = (f32[5,1,8,128]{3,2,1,0:T(8,128)S(1)}, f32[5,1,8,128]{3,2,1,0:T(8,128)S(1)}, u32[]{:S(2)}, u32[]{:S(2)}) collective-permute-start(f32[5,1,8,128]{3,2,1,0:T(8,128)S(1)} %get-tuple-element.154), channel_id=1, source_target_pairs={{32,0},{64,32},{96,64},{128,96},{160,128},{192,160},{224,192},{256... | collective-permute-start | bytes 61448 | tf_op jit(solution)/shard_map/ppermute | solution.py:42
  130.3 8.8 %collective-permute-start.12 = (s32[4]{0:T(128)S(1)}, s32[4]{0:T(128)S(1)}, u32[]{:S(2)}, u32[]{:S(2)}) collective-permute-start(s32[4]{0:T(128)S(1)} %copy-done.39), channel_id=1, source_target_pairs={{96,0},{128,32},{160,64},{192,96},{224,128},{256,160},{288,192},{3... | collective-permute-start | bytes 56 | tf_op jit(solution)/shard_map/ppermute | solution.py:52
  132.3 50.5 %copy-start.6 = (f32[5,1,8,128]{3,2,1,0:T(8,128)}, f32[5,1,8,128]{3,2,1,0:T(8,128)S(1)}, u32[]{:S(2)}) copy-start(f32[5,1,8,128]{3,2,1,0:T(8,128)S(1)} %collective-permute-done.7) | copy-start | bytes 61444
  132.3 11.7 %collective-permute-start.13 = (f32[4,1536]{1,0:T(4,128)S(1)}, f32[4,1536]{1,0:T(4,128)S(1)}, u32[]{:S(2)}, u32[]{:S(2)}) collective-permute-start(f32[4,1536]{1,0:T(4,128)S(1)} %get-tuple-element.76), channel_id=1, source_target_pairs={{96,0},{128,32},{160,64},{192,96},{224,128},{256,160},{288,192},{3... | collective-permute-start | bytes 73736 | tf_op jit(solution)/shard_map/ppermute | solution.py:52
  139.1 8.7 %collective-permute-start.16 = (s32[4]{0:T(128)S(1)}, s32[4]{0:T(128)S(1)}, u32[]{:S(2)}, u32[]{:S(2)}) collective-permute-start(s32[4]{0:T(128)S(1)} %copy-done.38), channel_id=1, source_target_pairs={{32,0},{64,32},{96,64},{128,96},{160,128},{192,160},{224,192},{256... | collective-permute-start | bytes 56 | tf_op jit(solution)/shard_map/ppermute | solution.py:52
  144.0 5.9 %collective-permute-start.17 = (f32[4,1536]{1,0:T(4,128)S(1)}, f32[4,1536]{1,0:T(4,128)S(1)}, u32[]{:S(2)}, u32[]{:S(2)}) collective-permute-start(f32[4,1536]{1,0:T(4,128)S(1)} %get-tuple-element.75), channel_id=1, source_target_pairs={{32,0},{64,32},{96,64},{128,96},{160,128},{192,160},{224,192},{256... | collective-permute-start | bytes 73736 | tf_op jit(solution)/shard_map/ppermute | solution.py:52
  147.9 10.9 %collective-permute-start.18 = (s32[4]{0:T(128)S(1)}, s32[4]{0:T(128)S(1)}, u32[]{:S(2)}, u32[]{:S(2)}) collective-permute-start(s32[4]{0:T(128)S(1)} %copy-done.37), channel_id=1, source_target_pairs={{0,32},{32,64},{64,96},{96,128},{128,160},{160,192},{192,224},{224... | collective-permute-start | bytes 56 | tf_op jit(solution)/shard_map/ppermute | solution.py:52
  149.8 12.2 %collective-permute-start.19 = (f32[4,1536]{1,0:T(4,128)S(1)}, f32[4,1536]{1,0:T(4,128)S(1)}, u32[]{:S(2)}, u32[]{:S(2)}) collective-permute-start(f32[4,1536]{1,0:T(4,128)S(1)} %get-tuple-element.74), channel_id=1, source_target_pairs={{0,32},{32,64},{64,96},{96,128},{128,160},{160,192},{192,224},{224... | collective-permute-start | bytes 73736 | tf_op jit(solution)/shard_map/ppermute | solution.py:52
  158.8 22.8 %collective-permute-start.15 = (f32[4,1536]{1,0:T(4,128)S(1)}, f32[4,1536]{1,0:T(4,128)S(1)}, u32[]{:S(2)}, u32[]{:S(2)}) collective-permute-start(f32[4,1536]{1,0:T(4,128)S(1)} %get-tuple-element.71), channel_id=1, source_target_pairs={{64,0},{96,32},{128,64},{160,96},{192,128},{224,160},{256,192},{28... | collective-permute-start | bytes 73736 | tf_op jit(solution)/shard_map/ppermute | solution.py:52
  162.0 11.8 %collective-permute-start.21 = (f32[4,1536]{1,0:T(4,128)S(1)}, f32[4,1536]{1,0:T(4,128)S(1)}, u32[]{:S(2)}, u32[]{:S(2)}) collective-permute-start(f32[4,1536]{1,0:T(4,128)S(1)} %get-tuple-element.73), channel_id=1, source_target_pairs={{0,64},{32,96},{64,128},{96,160},{128,192},{160,224},{192,256},{22... | collective-permute-start | bytes 73736 | tf_op jit(solution)/shard_map/ppermute | solution.py:52
  168.8 12.0 %collective-permute-start.23 = (f32[4,1536]{1,0:T(4,128)S(1)}, f32[4,1536]{1,0:T(4,128)S(1)}, u32[]{:S(2)}, u32[]{:S(2)}) collective-permute-start(f32[4,1536]{1,0:T(4,128)S(1)} %get-tuple-element.72), channel_id=1, source_target_pairs={{0,96},{32,128},{64,160},{96,192},{128,224},{160,256},{192,288},{2... | collective-permute-start | bytes 73736 | tf_op jit(solution)/shard_map/ppermute | solution.py:52
  173.8 22.9 %collective-permute-start.8 = (f32[5,10,1,128]{3,2,1,0:T(1,128)}, f32[5,10,1,128]{3,2,1,0:T(1,128)}, u32[]{:S(2)}, u32[]{:S(2)}) collective-permute-start(f32[5,10,1,128]{3,2,1,0:T(1,128)} %get-tuple-element.65), channel_id=1, source_target_pairs={{0,8},{8,16},{16,24},{1,9},{9,17},{17,25},{2,10},{10,18},{18,26},{... | collective-permute-start | bytes 76808 | tf_op jit(solution)/shard_map/ppermute | solution.py:40
  179.3 17.4 %collective-permute-start.9 = (f32[5,10,1,128]{3,2,1,0:T(1,128)}, f32[5,10,1,128]{3,2,1,0:T(1,128)}, u32[]{:S(2)}, u32[]{:S(2)}) collective-permute-start(f32[5,10,1,128]{3,2,1,0:T(1,128)} %get-tuple-element.66), channel_id=1, source_target_pairs={{8,0},{16,8},{24,16},{9,1},{17,9},{25,17},{10,2},{18,10},{26,18},{... | collective-permute-start | bytes 76808 | tf_op jit(solution)/shard_map/ppermute | solution.py:42
  184.8 26.4 %copy-start.35 = (f32[5]{0:T(128)S(1)}, f32[5]{0:T(128)}, u32[]{:S(2)}) copy-start(f32[5]{0:T(128)} %constant.102.clone) | copy-start | bytes 64
  184.8 20.5 %collective-permute-start.31 = (f32[4,1,8,128]{3,1,2,0:T(1,128)S(1)}, f32[4,1,8,128]{3,1,2,0:T(1,128)S(1)}, u32[]{:S(2)}, u32[]{:S(2)}) collective-permute-start(f32[4,1,8,128]{3,1,2,0:T(1,128)S(1)} %get-tuple-element.167), channel_id=1, source_target_pairs={{0,32},{32,64},{64,96},{96,128},{128,160},{160,192},{192,224},{224... | collective-permute-start | bytes 49160 | tf_op jit(solution)/shard_map/ppermute | solution.py:40
  186.8 18.6 %collective-permute-start.30 = (f32[4,1,8,128]{3,1,2,0:T(1,128)S(1)}, f32[4,1,8,128]{3,1,2,0:T(1,128)S(1)}, u32[]{:S(2)}, u32[]{:S(2)}) collective-permute-start(f32[4,1,8,128]{3,1,2,0:T(1,128)S(1)} %get-tuple-element.168), channel_id=1, source_target_pairs={{32,0},{64,32},{96,64},{128,96},{160,128},{192,160},{224,192},{256... | collective-permute-start | bytes 49160 | tf_op jit(solution)/shard_map/ppermute | solution.py:42
  197.8 13.4 %collective-permute-start.11 = (f32[5,10,10,1]{3,2,1,0:T(8,128)S(1)}, f32[5,10,10,1]{3,2,1,0:T(8,128)S(1)}, u32[]{:S(2)}, u32[]{:S(2)}) collective-permute-start(f32[5,10,10,1]{3,2,1,0:T(8,128)S(1)} %get-tuple-element.53), channel_id=1, source_target_pairs={{1,0},{2,1},{3,2},{4,3},{5,4},{6,5},{7,6},{9,8},{10,9},{11,10},{12... | collective-permute-start | bytes 6008 | tf_op jit(solution)/shard_map/ppermute | solution.py:42
  199.7 11.5 %collective-permute-start.10 = (f32[5,10,10,1]{3,2,1,0:T(8,128)S(1)}, f32[5,10,10,1]{3,2,1,0:T(8,128)S(1)}, u32[]{:S(2)}, u32[]{:S(2)}) collective-permute-start(f32[5,10,10,1]{3,2,1,0:T(8,128)S(1)} %get-tuple-element.54), channel_id=1, source_target_pairs={{0,1},{1,2},{2,3},{3,4},{4,5},{5,6},{6,7},{8,9},{9,10},{10,11},{11... | collective-permute-start | bytes 6008 | tf_op jit(solution)/shard_map/ppermute | solution.py:40
  205.4 10.6 %collective-permute-start.33 = (f32[4,10,1,128]{3,1,2,0:T(8,128)S(1)}, f32[4,10,1,128]{3,1,2,0:T(8,128)S(1)}, u32[]{:S(2)}, u32[]{:S(2)}) collective-permute-start(f32[4,10,1,128]{3,1,2,0:T(8,128)S(1)} %get-tuple-element.97), channel_id=1, source_target_pairs={{0,8},{8,16},{16,24},{1,9},{9,17},{17,25},{2,10},{10,18},{18,26},{... | collective-permute-start | bytes 61448 | tf_op jit(solution)/shard_map/ppermute | solution.py:40
  209.9 6.0 %collective-permute-start.32 = (f32[4,10,1,128]{3,1,2,0:T(8,128)S(1)}, f32[4,10,1,128]{3,1,2,0:T(8,128)S(1)}, u32[]{:S(2)}, u32[]{:S(2)}) collective-permute-start(f32[4,10,1,128]{3,1,2,0:T(8,128)S(1)} %get-tuple-element.98), channel_id=1, source_target_pairs={{8,0},{16,8},{24,16},{9,1},{17,9},{25,17},{10,2},{18,10},{26,18},{... | collective-permute-start | bytes 61448 | tf_op jit(solution)/shard_map/ppermute | solution.py:42
  216.2 15.8 %copy-start.9 = (f32[1,8,8,128]{3,2,1,0:T(8,128)S(1)}, f32[1,8,8,128]{3,2,1,0:T(8,128)}, u32[]{:S(2)}) copy-start(f32[1,8,8,128]{3,2,1,0:T(8,128)} %copy-done.8) | copy-start | bytes 98308
  216.2 9.8 %collective-permute-start.35 = (f32[4,10,10,1]{3,1,2,0:T(8,128)S(1)}, f32[4,10,10,1]{3,1,2,0:T(8,128)S(1)}, u32[]{:S(2)}, u32[]{:S(2)}) collective-permute-start(f32[4,10,10,1]{3,1,2,0:T(8,128)S(1)} %get-tuple-element.57), channel_id=1, source_target_pairs={{0,1},{1,2},{2,3},{3,4},{4,5},{5,6},{6,7},{8,9},{9,10},{10,11},{11... | collective-permute-start | bytes 4808 | tf_op jit(solution)/shard_map/ppermute | solution.py:40
  221.4 10.2 %collective-permute-start.34 = (f32[4,10,10,1]{3,1,2,0:T(8,128)S(1)}, f32[4,10,10,1]{3,1,2,0:T(8,128)S(1)}, u32[]{:S(2)}, u32[]{:S(2)}) collective-permute-start(f32[4,10,10,1]{3,1,2,0:T(8,128)S(1)} %get-tuple-element.58), channel_id=1, source_target_pairs={{1,0},{2,1},{3,2},{4,3},{5,4},{6,5},{7,6},{9,8},{10,9},{11,10},{12... | collective-permute-start | bytes 4808 | tf_op jit(solution)/shard_map/ppermute | solution.py:42
  (32 other events, 112.4 us)
where the time goes:
time: 236 us; the launch traced here: 234 us
  starting transfers between devices  146 us (62%)
  waiting for transfers between devices  47.3 us (20%)
  other arithmetic  14.2 us (6%)
  local copies, waits for them, and re-layouts  13 us (6%)
  matrix products  10.9 us (5%)
    ppermute x12, starting transfers between devices, from_behind(): return lax.ppermute(block, axis, route)  53.6 us
    ppermute x12, starting transfers between devices, padded_2(): lax.ppermute(head, axis, [((i + 1) % count, i) for i in range(ends)])  46.8 us
    ppermute x12, starting transfers between devices, padded_2(): lax.ppermute(tail, axis, [(i, (i + 1) % count) for i in range(ends)])  45.8 us
    ppermute x12, waiting for transfers between devices, padded_2(): lax.ppermute(head, axis, [((i + 1) % count, i) for i in range(ends)])  18.4 us
    ppermute x12, waiting for transfers between devices, padded_2(): lax.ppermute(tail, axis, [(i, (i + 1) % count) for i in range(ends)])  16 us
    ppermute x12, waiting for transfers between devices, from_behind(): return lax.ppermute(block, axis, route)  12.9 us
  transfers between devices with their start and end apart: 36, of which 13 were waited for; matrix products, arithmetic and copies ran while one was open for 13% of the time, Pallas kernels for 0%

commit v1 on v0

v1 whole, which is shorter than its diff:
```python
import functools

import jax
import jax.numpy as jnp
import numpy as np
from jax import lax
from jax.experimental import pallas as pl
from jax.experimental.pallas import tpu as pltpu
from jax.sharding import PartitionSpec as P

MESH = pl.DeviceIdType.MESH
F32 = jnp.float32
BF16 = jnp.bfloat16

lobatto_points = np.array(
    [
        -1.0,
        -0.8717401485096066,
        -0.5917001814331423,
        -0.2092992179024789,
        0.2092992179024789,
        0.5917001814331423,
        0.8717401485096066,
        1.0,
    ]
)
flux_half = 0.08
gamma_less = 0.4
acoustic_step = 0.01
upwind_speed = 1.5
face_lift = 28.0
REACH = 3
WINDOW = 4


def derivative_matrix():
    points = lobatto_points
    gaps = points[:, None] - points[None, :] + np.eye(8)
    products = np.prod(gaps, axis=1)
    matrix = products[:, None] / (products[None, :] * gaps)
    np.fill_diagonal(matrix, 0.0)
    np.fill_diagonal(matrix, -matrix.sum(axis=1))
    return matrix


def derivative_operands():
    deriv = derivative_matrix()
    eye = np.eye(8)
    along_xy = np.concatenate([np.kron(deriv, eye), np.kron(eye, deriv)], axis=1)
    along_z = np.kron(np.eye(16), deriv.T)
    whole = np.concatenate([along_xy, along_z], axis=0).astype(np.float32)
    high = whole.astype(jnp.bfloat16)
    low = (whole - high.astype(np.float32)).astype(jnp.bfloat16)
    return np.stack([high, low])


def split(value):
    high = value.astype(BF16)
    return high, (value - high.astype(F32)).astype(BF16)


def dot_nn(left, right):
    return lax.dot_general(left, right, (((1,), (0,)), ((), ())), preferred_element_type=F32)


def dot_nt(left, right):
    return lax.dot_general(left, right, (((1,), (1,)), ((), ())), preferred_element_type=F32)


def lanes(shape):
    return lax.broadcasted_iota(jnp.int32, shape, len(shape) - 1)


def rows(shape):
    return lax.broadcasted_iota(jnp.int32, shape, len(shape) - 2)


class Halo:
    def __init__(self, x_ref, y_ref, z_ref, first):
        self.x_ref, self.y_ref, self.z_ref, self.first = x_ref, y_ref, z_ref, first

    def face(self, component, axis, side):
        at = self.first + component
        if axis == 0:
            return self.x_ref[side, at]
        if axis == 1:
            return self.y_ref[side, at]
        face = self.z_ref[side]
        return [jnp.broadcast_to(face[:, 8 * at + x : 8 * at + x + 1], (8, 128)) for x in range(8)]

    def shifted(self, field, component, axis, side):
        return shift(field, self.face(component, axis, side), axis, side)


def shift(field, face, axis, side):
    if axis == 0:
        if side == 0:
            return jnp.concatenate([face[None], field[:-1]], axis=0)
        return jnp.concatenate([field[1:], face[None]], axis=0)
    if axis == 1:
        rolled = pltpu.roll(field, 1 if side == 0 else 7, 1)
        edge = rows((8, 8, 128)) == (0 if side == 0 else 7)
        return jnp.where(edge, jnp.broadcast_to(face[:, None, :], (8, 8, 128)), rolled)
    rolled = pltpu.roll(field, 1 if side == 0 else 127, 2)
    edge = lanes((8, 8, 128)) == (0 if side == 0 else 127)
    return jnp.where(edge, jnp.stack(face), rolled)


def les_rate(state, halo):
    total = [-6.0 * part for part in state]
    for axis in range(3):
        for side in range(2):
            near = [halo.shifted(state[c], c, axis, side) for c in range(5)]
            momentum = near[1:4]
            energy = near[4] + 2.5
            inverse = 1.0 / (near[0] + 1.0)
            square = (
                momentum[0] * momentum[0] + momentum[1] * momentum[1] + momentum[2] * momentum[2]
            )
            pressure = gamma_less * (energy - 0.5 * (square * inverse))
            speed = momentum[axis] * inverse
            flux = [momentum[axis]]
            for component in range(3):
                term = momentum[component] * speed
                flux.append(term + pressure if component == axis else term)
            flux.append((energy + pressure) * speed)
            for c in range(5):
                total[c] = total[c] + (near[c] + flux[c] if side == 0 else near[c] - flux[c])
    return [flux_half * part for part in total]


def lamb_vector(state, halo):
    inverse = 1.0 / (state[0] + 1.0)
    velocity = [state[1 + c] * inverse for c in range(3)]
    packed = []
    for side in range(2):
        face = halo.z_ref[side]
        inverse_face = 1.0 / (face + 1.0)
        packed.append([face * pltpu.roll(inverse_face, 8 * (1 + c), 1) for c in range(3)])

    def near(component, axis, side):
        if axis == 2:
            face = packed[side][component]
            start = 8 * (1 + component)
            face = [jnp.broadcast_to(face[:, start + x : start + x + 1], (8, 128)) for x in range(8)]
        else:
            face = halo.face(1 + component, axis, side) / (halo.face(0, axis, side) + 1.0)
        return shift(velocity[component], face, axis, side)

    def slope(component, axis):
        return 0.5 * (near(component, axis, 1) - near(component, axis, 0))

    vort_x = slope(2, 1) - slope(1, 2)
    vort_y = slope(0, 2) - slope(2, 0)
    vort_z = slope(1, 0) - slope(0, 1)
    return [
        vort_y * velocity[2] - vort_z * velocity[1],
        vort_z * velocity[0] - vort_x * velocity[2],
        vort_x * velocity[1] - vort_y * velocity[0],
    ]


def flux_along(state, mean_speed, axis):
    flux = [mean_speed[axis] * state[0] + state[1 + axis]]
    for component in range(3):
        term = mean_speed[axis] * state[1 + component]
        flux.append(term + state[0] if component == axis else term)
    return flux


def acoustic_rate(state, mean_speed, halo, deriv_ref):
    flux_x = flux_along(state, mean_speed, 0)
    flux_y = flux_along(state, mean_speed, 1)
    flux_z = flux_along(state, mean_speed, 2)
    high = deriv_ref[0]
    low = deriv_ref[1]
    columns = jnp.concatenate(
        [
            jnp.concatenate([flux_x[c].reshape(64, 128), flux_y[c].reshape(64, 128)], axis=0)
            for c in range(4)
        ],
        axis=1,
    )
    column_high, column_low = split(columns)
    slopes_xy = (
        dot_nn(high[:64], column_high) + dot_nn(high[:64], column_low) + dot_nn(low[:64], column_high)
    )
    lines = jnp.concatenate([flux_z[c].reshape(64, 128) for c in range(4)], axis=0)
    line_high, line_low = split(lines)
    slopes_z = (
        dot_nn(line_high, high[64:]) + dot_nn(line_low, high[64:]) + dot_nn(line_high, low[64:])
    )
    total = [
        -(slopes_xy[:, 128 * c : 128 * c + 128] + slopes_z[64 * c : 64 * c + 64]).reshape(8, 8, 128)
        for c in range(4)
    ]
    half_lift = 0.5 * face_lift
    upwind_lift = half_lift * upwind_speed
    for side in range(2):
        plane = 0 if side == 0 else 7
        jump = [halo.face(c, 0, side) - state[c][plane] for c in range(4)]
        flux = flux_along(jump, [mean_speed[0][plane], None, None], 0)
        sign = half_lift if side == 0 else -half_lift
        for c in range(4):
            lifted = (sign * flux[c] + upwind_lift * jump[c])[None]
            zeros = jnp.zeros((7, 8, 128), F32)
            parts = [lifted, zeros] if side == 0 else [zeros, lifted]
            total[c] = total[c] + jnp.concatenate(parts, axis=0)
    for axis in (1, 2):
        position = rows((8, 8, 128)) if axis == 1 else lanes((8, 8, 128)) % 8
        is_left, is_right = position == 0, position == 7
        jump = []
        for c in range(4):
            if axis == 1:
                lower = jnp.broadcast_to(halo.face(c, 1, 0)[:, None, :], (8, 8, 128))
                upper = jnp.broadcast_to(halo.face(c, 1, 1)[:, None, :], (8, 8, 128))
            else:
                lower = halo.shifted(state[c], c, 2, 0)
                upper = halo.shifted(state[c], c, 2, 1)
            other = jnp.where(is_left, lower, jnp.where(is_right, upper, state[c]))
            jump.append(other - state[c])
        flux = flux_along(jump, mean_speed, axis)
        sign = jnp.where(is_left, half_lift, -half_lift)
        for c in range(4):
            total[c] = total[c] + (sign * flux[c] + upwind_lift * jump[c])
    return total


def pack_faces_z(planes, side):
    face = jnp.zeros((8, 128), F32)
    lane = lanes((8, 128))
    at = 0 if side == 0 else 127
    for n, plane in enumerate(planes):
        face = jnp.where(lane == n, jnp.broadcast_to(plane[:, at : at + 1], (8, 128)), face)
    return face


def quarter_transpose(groups, target):
    lane = lanes(groups[0].shape) // 32
    result = None
    for g, group in enumerate(groups):
        moved = group if g == target else pltpu.roll(group, (32 * (g - target)) % 128, 1)
        result = moved if result is None else jnp.where(lane == g, moved, result)
    return result


def projection_operands(proj_ref):
    lane = lanes((8, 128))
    row = rows((8, 128))
    tile = jnp.zeros((8, 128), F32)
    for k in range(8):
        for e in range(8):
            tile = jnp.where((row == k) & (lane % 8 == e), proj_ref[k, e], tile)
    pieces = []
    for i in range(8):
        weight = jnp.zeros((8, 128), F32)
        for a in range(8):
            weight = jnp.where(lane % 64 // 8 == a, proj_ref[i, a], weight)
        pieces.append(weight * tile)
    return tile, jnp.concatenate(pieces, axis=0)


def place_operands(tile, own_ref, slot_ref, start):
    lane = lanes((8, 128))
    row = rows((8, 128))
    block = lane // 8
    owner = jnp.zeros((8, 128), jnp.int32)
    slot = jnp.zeros((8, 128), jnp.int32)
    for b in range(16):
        owner = jnp.where(block == b, own_ref[0, 0, b], owner)
        slot = jnp.where(block == b, slot_ref[0, 0, b], slot)
    rank = jnp.zeros((8, 128), jnp.int32)
    for b in range(16):
        rank = rank + jnp.where((owner == own_ref[0, 0, b]) & (block > b), 1, 0)
    place = (owner - start) * WINDOW + rank
    columns = jnp.concatenate([jnp.where(place == n, tile, 0.0) for n in range(16)], axis=0)
    same = (lane % 8) == row
    picks = jnp.concatenate(
        [jnp.where((place == n) & same, 1.0, 0.0) for n in range(16)], axis=0
    )
    labels = dot_nt(slot.astype(F32).astype(BF16), picks.astype(BF16))
    return columns, labels


def kernel(
    sizes,
    les,
    ac,
    mf,
    proj,
    own,
    slot,
    deriv,
    les_out,
    src_out,
    ac_out,
    les_v,
    ac_v,
    mf_v,
    deriv_v,
    send_y,
    send_z,
    halo_x,
    halo_y,
    halo_z,
    pieces,
    arrived,
    sec_v,
    sec_send_y,
    sec_send_z,
    sec_halo_x,
    sec_halo_y,
    sec_halo_z,
    mid_v,
    mid_send_y,
    mid_send_z,
    mid_halo_x,
    mid_halo_y,
    mid_halo_z,
    rate_v,
    slope_v,
    les_next,
    src_v,
    ac_next,
    load_sem,
    out_sem,
    send_sem,
    recv_sem,
    piece_send,
    piece_recv,
):
    names = ("gx", "gy", "gz")
    at = [lax.axis_index(name) for name in names]
    me = at[0]
    count_x = sizes[0]

    def exists(axis, distance):
        other = at[axis] + distance
        return (other >= 0) & (other < sizes[axis])

    barrier = pltpu.get_barrier_semaphore()
    expected = jnp.int32(0)
    for axis, reach in ((0, REACH), (1, 1), (2, 1)):
        for distance in range(-reach, reach + 1):
            if distance == 0:
                continue
            near = exists(axis, distance)

            @pl.when(near)
            def _():
                pl.semaphore_signal(
                    barrier,
                    inc=1,
                    device_id={names[axis]: at[axis] + distance},
                    device_id_type=MESH,
                )

            expected = expected + jnp.where(near, 1, 0)

    loads = [
        pltpu.make_async_copy(source, target, load_sem.at[n])
        for n, (source, target) in enumerate(
            ((les, les_v), (ac, ac_v), (mf, mf_v), (deriv, deriv_v))
        )
    ]
    for load in loads:
        load.start()

    def start_of(index):
        return (index * (count_x - (WINDOW - 1))) // count_x

    start = start_of(me)

    def comes(distance):
        other = me + distance
        begin = start_of(other)
        return exists(0, distance) & (begin <= me) & (me < begin + WINDOW)

    for side, distance in ((0, -1), (1, 1)):
        for axis, refs in (
            (0, (halo_x, sec_halo_x, mid_halo_x)),
            (1, (halo_y, sec_halo_y, mid_halo_y)),
            (2, (halo_z, sec_halo_z, mid_halo_z)),
        ):

            @pl.when(jnp.logical_not(exists(axis, distance)))
            def _():
                for ref in refs:
                    ref[side] = jnp.zeros(ref.shape[1:], F32)

    for distance in range(-REACH, REACH + 1):
        if distance != 0:

            @pl.when(jnp.logical_not(comes(distance)))
            def _():
                arrived[distance + REACH] = jnp.zeros((56, 128), F32)

    def message(source, target, axis, side, slot_index):
        distance = -1 if side == 0 else 1
        return pltpu.make_async_remote_copy(
            src_ref=source,
            dst_ref=target,
            send_sem=send_sem.at[slot_index],
            recv_sem=recv_sem.at[slot_index],
            device_id={names[axis]: at[axis] + distance},
            device_id_type=MESH,
        )

    def begin(entries):
        for source, target, axis, side, slot_index in entries:

            @pl.when(exists(axis, -1 if side == 0 else 1))
            def _():
                message(source, target, axis, side, slot_index).start()

    def arrive(entries):
        for source, target, axis, side, slot_index in entries:
            @pl.when(exists(axis, 1 if side == 0 else -1))
            def _():
                message(source, target, axis, side, slot_index).wait_recv()

    def drain(entries):
        for source, target, axis, side, slot_index in entries:

            @pl.when(exists(axis, -1 if side == 0 else 1))
            def _():
                message(source, target, axis, side, slot_index).wait_send()

    flow_x = [
        (les.at[:, 0 if side == 0 else 7], halo_x.at[1 - side, 0:5], 0, side, side)
        for side in range(2)
    ]
    sound_x = [
        (ac.at[:, 0 if side == 0 else 7], halo_x.at[1 - side, 5:9], 0, side, 2 + side)
        for side in range(2)
    ]
    near_yz = [
        (send_y.at[side], halo_y.at[1 - side], 1, side, 4 + side) for side in range(2)
    ] + [(send_z.at[side], halo_z.at[1 - side], 2, side, 6 + side) for side in range(2)]
    section = (
        [
            (sec_v.at[:, 0 if side == 0 else 7], sec_halo_x.at[1 - side], 0, side, 8 + side)
            for side in range(2)
        ]
        + [
            (sec_send_y.at[side], sec_halo_y.at[1 - side], 1, side, 10 + side)
            for side in range(2)
        ]
        + [
            (sec_send_z.at[side], sec_halo_z.at[1 - side], 2, side, 12 + side)
            for side in range(2)
        ]
    )
    middle = (
        [
            (mid_v.at[:, 0 if side == 0 else 7], mid_halo_x.at[1 - side], 0, side, 14 + side)
            for side in range(2)
        ]
        + [
            (mid_send_y.at[side], mid_halo_y.at[1 - side], 1, side, 16 + side)
            for side in range(2)
        ]
        + [
            (mid_send_z.at[side], mid_halo_z.at[1 - side], 2, side, 18 + side)
            for side in range(2)
        ]
    )

    for load in loads[:2]:
        load.wait()
    for side in range(2):
        row = 0 if side == 0 else 7
        send_y[side, 0:5] = les_v[:, :, row, :]
        send_y[side, 5:9] = ac_v[:, :, row, :]
        send_z[side] = pack_faces_z(
            [les_v[c, x] for c in range(5) for x in range(8)]
            + [ac_v[c, x] for c in range(4) for x in range(8)],
            side,
        )

    pl.semaphore_wait(barrier, expected)
    begin(flow_x)
    begin(near_yz)
    begin(sound_x)

    tile, plane_weights = projection_operands(proj)
    weight_high, weight_low = split(plane_weights)
    plane_operand = jnp.concatenate([weight_high, weight_low], axis=1)
    columns, labels = place_operands(tile, own, slot, start)
    column_high, column_low = split(columns)
    column_operand = jnp.concatenate(
        [
            jnp.concatenate([column_high, column_high], axis=1),
            jnp.concatenate([column_low, column_low], axis=1),
        ],
        axis=0,
    )
    for w in range(WINDOW):
        pieces[w, 48:56] = quarter_transpose([labels] * 4, w)
    for load in loads[2:]:
        load.wait()

    state = [les_v[c] for c in range(5)]
    halo = Halo(halo_x, halo_y, halo_z, 0)
    arrive(near_yz)
    arrive(flow_x)
    lamb = lamb_vector(state, halo)
    cells = jnp.concatenate([part.reshape(64, 128) for part in lamb], axis=1)
    cell_high, cell_low = split(cells)
    stacked = jnp.concatenate([cell_high, cell_low, cell_high, cell_low], axis=0)
    planes = dot_nn(plane_operand, stacked)
    planes = jnp.concatenate([planes[:, 128 * c : 128 * c + 128] for c in range(3)], axis=0)
    plane_high, plane_low = split(planes)
    both = dot_nt(jnp.concatenate([plane_high, plane_low], axis=1), column_operand)
    placed = both[:, :128] + both[:, 128:]
    groups = [placed[48 * g : 48 * g + 48] for g in range(4)]
    for w in range(WINDOW):
        pieces[w, 0:48] = quarter_transpose(groups, w)

    def piece_copy(w):
        target = start + w
        slot_index = me - target + REACH
        return pltpu.make_async_remote_copy(
            src_ref=pieces.at[w],
            dst_ref=arrived.at[slot_index],
            send_sem=piece_send.at[w],
            recv_sem=piece_recv.at[slot_index],
            device_id={"gx": target},
            device_id_type=MESH,
        )

    for w in range(WINDOW):

        @pl.when(start + w != me)
        def _():
            piece_copy(w).start()

    arrived[REACH] = pieces[me - start]

    rate = les_rate(state, halo)
    for c in range(5):
        rate_v[c] = rate[c]
        sec_v[c] = state[c] + rate[c]
    for side in range(2):
        sec_send_y[side] = sec_v[:, :, 0 if side == 0 else 7, :]
        sec_send_z[side] = pack_faces_z(
            [sec_v[c, x] for c in range(5) for x in range(8)], side
        )
    begin(section)

    mean_speed = [mf_v[c] for c in range(3)]
    arrive(sound_x)
    sound = [ac_v[c] for c in range(4)]
    slopes = acoustic_rate(sound, mean_speed, Halo(halo_x, halo_y, halo_z, 5), deriv_v)
    for c in range(4):
        slope_v[c] = slopes[c]

    for distance in range(-REACH, REACH + 1):
        if distance != 0:

            @pl.when(comes(distance))
            def _():
                pltpu.make_async_remote_copy(
                    src_ref=pieces.at[0],
                    dst_ref=arrived.at[distance + REACH],
                    send_sem=piece_send.at[0],
                    recv_sem=piece_recv.at[distance + REACH],
                    device_id={"gx": me + distance},
                    device_id_type=MESH,
                ).wait_recv()

    halves = []
    tags = []
    zero = jnp.zeros((48, 128), F32)
    for half in range(2):
        members = [4 * half + n for n in range(4)]
        parts = [arrived[n, 0:48] if n < 7 else zero for n in members]
        quarter = [quarter_transpose(parts, g) for g in range(4)]
        halves.append(jnp.concatenate(quarter, axis=0))
        tag = jnp.zeros((8, 128), F32)
        for n in members:
            if n < 7:
                tag = jnp.where(lanes((8, 128)) // 32 == n % 4, arrived[n, 48:56], tag)
        tags.append(tag)
    same = (lanes((8, 128)) % 8) == rows((8, 128))
    picks = jnp.concatenate(
        [
            jnp.concatenate(
                [jnp.where((tag == float(s)) & same, 1.0, 0.0) for s in range(16)], axis=0
            )
            for tag in tags
        ],
        axis=1,
    ).astype(BF16)
    gathered = jnp.concatenate(halves, axis=1)
    gathered_high, gathered_low = split(gathered)
    source = dot_nt(gathered_high, picks) + dot_nt(gathered_low, picks)
    source = source.reshape(3, 8, 8, 128)
    src_v[...] = source
    for c in range(4):
        if c > 0:
            slope_v[c] = slope_v[c] + src_v[c - 1]
        mid_v[c] = ac_v[c] + acoustic_step * slope_v[c]
    for side in range(2):
        mid_send_y[side] = mid_v[:, :, 0 if side == 0 else 7, :]
        mid_send_z[side] = pack_faces_z(
            [mid_v[c, x] for c in range(4) for x in range(8)], side
        )
    begin(middle)
    src_copy = pltpu.make_async_copy(src_v, src_out, out_sem.at[1])
    src_copy.start()

    arrive(section)
    rate = les_rate([sec_v[c] for c in range(5)], Halo(sec_halo_x, sec_halo_y, sec_halo_z, 0))
    for c in range(5):
        les_next[c] = les_v[c] + 0.5 * (rate_v[c] + rate[c])
    les_copy = pltpu.make_async_copy(les_next, les_out, out_sem.at[0])
    les_copy.start()

    arrive(middle)
    slopes = acoustic_rate(
        [mid_v[c] for c in range(4)],
        [mf_v[c] for c in range(3)],
        Halo(mid_halo_x, mid_halo_y, mid_halo_z, 0),
        deriv_v,
    )
    for c in range(4):
        total = slope_v[c] + slopes[c]
        if c > 0:
            total = total + src_v[c - 1]
        ac_next[c] = ac_v[c] + 0.5 * acoustic_step * total
    ac_copy = pltpu.make_async_copy(ac_next, ac_out, out_sem.at[2])
    ac_copy.start()

    drain(flow_x)
    drain(sound_x)
    drain(near_yz)
    drain(section)
    drain(middle)
    for w in range(WINDOW):

        @pl.when(start + w != me)
        def _():
            piece_copy(w).wait_send()

    src_copy.wait()
    les_copy.wait()
    ac_copy.wait()


def local(les_state, acoustic_state, mean_flow, projection, target_owner, target_slot):
    sizes = tuple(lax.axis_size(name) for name in ("gx", "gy", "gz"))
    deriv = jnp.asarray(derivative_operands())
    anywhere = pl.BlockSpec(memory_space=pl.ANY)
    scalars = pl.BlockSpec(memory_space=pltpu.SMEM)

    def vmem(*shape):
        return pltpu.VMEM(shape, F32)

    def halos(n):
        return [vmem(2, n, 8, 128), vmem(2, n, 8, 128), vmem(2, 8, 128)]

    field = (8, 8, 128)
    return pl.pallas_call(
        functools.partial(kernel, sizes),
        name="coupled_step",
        out_shape=(
            jax.ShapeDtypeStruct((5,) + field, F32),
            jax.ShapeDtypeStruct((3,) + field, F32),
            jax.ShapeDtypeStruct((4,) + field, F32),
        ),
        in_specs=[anywhere, anywhere, anywhere, scalars, scalars, scalars, anywhere],
        out_specs=(anywhere, anywhere, anywhere),
        scratch_shapes=[
            vmem(5, *field),
            vmem(4, *field),
            vmem(3, *field),
            pltpu.VMEM((2, 192, 128), BF16),
            vmem(2, 9, 8, 128),
            vmem(2, 8, 128),
            *halos(9),
            vmem(4, 56, 128),
            vmem(7, 56, 128),
            vmem(5, *field),
            vmem(2, 5, 8, 128),
            vmem(2, 8, 128),
            *halos(5),
            vmem(4, *field),
            vmem(2, 4, 8, 128),
            vmem(2, 8, 128),
            *halos(4),
            vmem(5, *field),
            vmem(4, *field),
            vmem(5, *field),
            vmem(3, *field),
            vmem(4, *field),
            pltpu.SemaphoreType.DMA((4,)),
            pltpu.SemaphoreType.DMA((3,)),
            pltpu.SemaphoreType.DMA((20,)),
            pltpu.SemaphoreType.DMA((20,)),
            pltpu.SemaphoreType.DMA((4,)),
            pltpu.SemaphoreType.DMA((7,)),
        ],
        compiler_params=pltpu.CompilerParams(collective_id=0, has_side_effects=True),
    )(les_state, acoustic_state, mean_flow, projection, target_owner, target_slot, deriv)


def solution(mesh):
    fields = P(None, "gx", "gy", "gz")
    blocks = P("gx", "gy", "gz")
    return jax.shard_map(
        local,
        mesh=mesh,
        in_specs=(fields, fields, fields, P(), blocks, blocks),
        out_specs=(fields, fields, fields),
        check_vma=False,
    )
```

time: 236 us -> 38.3 us (0.16)
  the two profiles are of different devices: /device:TPU:70 before, /device:TPU:1 now
where the time goes in v1:
time: 38.3 us; the launch traced here: 38.1 us
  Pallas kernels  34.2 us (89%)
  local copies, waits for them, and re-layouts  3.23 us (8%)
  between operations  0.65 us (2%)
    pallas_call x1, Pallas kernels, local(): pl.pallas_call(functools.partial(kernel, sizes), name='coupled_step', out...  34.2 us
    unnamed x7, local copies, waits for them, and re-layouts  3.23 us

profile of v1, /device:TPU:1, one launch (start us, length us, event | category | flops | bytes accessed | tf_op | source)
XLA Modules:
  0.0 38.1 jit_solution(2030764074060628280)
XLA Ops:
  0.6 34.2 %coupled_step.1 = (f32[5,8,8,128]{3,2,1,0:T(8,128)}, f32[3,8,8,128]{3,2,1,0:T(8,128)}, f32[4,8,8,128]{3,2,1,0:T(8,128)}) custom-call(f32[5,8,8,128]{3,2,1,0:T(8,128)} %les.1, f32[4,8,8,128]{3,2,1,0:T(8,128)} %ac.1, f32[3,8,8,128]{3,2,1,0:T(8,128)} %mf.1, f32[8,8]{1,0:T(8,128)} %proj.1, s32[1,1,16]{2,1,0:T(1,128)} %own.1, s32[1,1,16]{2,1,0:T(1,128)} %slot.1, ...), custom_call_target="tpu_custom_call" | custom-call | tf_op jit(solution)/shard_map/coupled_step/pallas_call | solution.py:664
  34.8 0.0 copy-start.1
  34.8 1.6 %copy.13 = f32[5,8,8,128]{3,2,1,0:T(8,128)} copy(f32[5,8,8,128]{3,2,1,0:T(8,128)} %get-tuple-element.6) | data formatting | bytes 327680
  36.5 0.0 copy-done.1
  36.5 0.0 copy-start
  36.5 0.6 %copy.14 = f32[3,8,8,128]{3,2,1,0:T(8,128)} copy(f32[3,8,8,128]{3,2,1,0:T(8,128)S(1)} %copy-done.1) | data formatting | bytes 196608
  37.1 0.3 copy-done
  37.4 0.7 %copy.15 = f32[4,8,8,128]{3,2,1,0:T(8,128)} copy(f32[4,8,8,128]{3,2,1,0:T(8,128)S(1)} %copy-done) | data formatting | bytes 262144
Async XLA Ops:
  34.8 1.6 %copy-start.1 = (f32[3,8,8,128]{3,2,1,0:T(8,128)S(1)}, f32[3,8,8,128]{3,2,1,0:T(8,128)}, u32[]{:S(2)}) copy-start(f32[3,8,8,128]{3,2,1,0:T(8,128)} %get-tuple-element.7) | copy-start | bytes 294916
  36.5 0.9 %copy-start = (f32[4,8,8,128]{3,2,1,0:T(8,128)S(1)}, f32[4,8,8,128]{3,2,1,0:T(8,128)}, u32[]{:S(2)}) copy-start(f32[4,8,8,128]{3,2,1,0:T(8,128)} %get-tuple-element.8) | copy-start | bytes 393220

commit v2 on v1

--- a/solution.py
+++ b/solution.py
@@ -287,13 +287,16 @@
     les,
     ac,
     mf,
+    proj_hbm,
+    own_hbm,
+    slot_hbm,
+    deriv,
+    les_next,
+    src_v,
+    ac_next,
     proj,
     own,
     slot,
-    deriv,
-    les_out,
-    src_out,
-    ac_out,
     les_v,
     ac_v,
     mf_v,
@@ -319,11 +322,7 @@
     mid_halo_z,
     rate_v,
     slope_v,
-    les_next,
-    src_v,
-    ac_next,
     load_sem,
-    out_sem,
     send_sem,
     recv_sem,
     piece_send,
@@ -360,7 +359,15 @@
     loads = [
         pltpu.make_async_copy(source, target, load_sem.at[n])
         for n, (source, target) in enumerate(
-            ((les, les_v), (ac, ac_v), (mf, mf_v), (deriv, deriv_v))
+            (
+                (les, les_v),
+                (ac, ac_v),
+                (proj_hbm, proj),
+                (own_hbm, own),
+                (slot_hbm, slot),
+                (mf, mf_v),
+                (deriv, deriv_v),
+            )
         )
     ]
     for load in loads:
@@ -466,6 +473,8 @@
         ]
     )
 
+    pl.semaphore_wait(barrier, expected)
+    begin(flow_x)
     for load in loads[:2]:
         load.wait()
     for side in range(2):
@@ -478,10 +487,10 @@
             side,
         )
 
-    pl.semaphore_wait(barrier, expected)
-    begin(flow_x)
     begin(near_yz)
     begin(sound_x)
+    for load in loads[2:]:
+        load.wait()
 
     tile, plane_weights = projection_operands(proj)
     weight_high, weight_low = split(plane_weights)
@@ -497,8 +506,6 @@
     )
     for w in range(WINDOW):
         pieces[w, 48:56] = quarter_transpose([labels] * 4, w)
-    for load in loads[2:]:
-        load.wait()
 
     state = [les_v[c] for c in range(5)]
     halo = Halo(halo_x, halo_y, halo_z, 0)
@@ -607,15 +614,11 @@
             [mid_v[c, x] for c in range(4) for x in range(8)], side
         )
     begin(middle)
-    src_copy = pltpu.make_async_copy(src_v, src_out, out_sem.at[1])
-    src_copy.start()
 
     arrive(section)
     rate = les_rate([sec_v[c] for c in range(5)], Halo(sec_halo_x, sec_halo_y, sec_halo_z, 0))
     for c in range(5):
         les_next[c] = les_v[c] + 0.5 * (rate_v[c] + rate[c])
-    les_copy = pltpu.make_async_copy(les_next, les_out, out_sem.at[0])
-    les_copy.start()
 
     arrive(middle)
     slopes = acoustic_rate(
@@ -629,8 +632,6 @@
         if c > 0:
             total = total + src_v[c - 1]
         ac_next[c] = ac_v[c] + 0.5 * acoustic_step * total
-    ac_copy = pltpu.make_async_copy(ac_next, ac_out, out_sem.at[2])
-    ac_copy.start()
 
     drain(flow_x)
     drain(sound_x)
@@ -643,9 +644,16 @@
         def _():
             piece_copy(w).wait_send()
 
-    src_copy.wait()
-    les_copy.wait()
-    ac_copy.wait()
+
+def write_out(les_v, src_v, ac_v, les_out, src_out, ac_out, sems):
+    copies = [
+        pltpu.make_async_copy(source, target, sems.at[n])
+        for n, (source, target) in enumerate(((les_v, les_out), (src_v, src_out), (ac_v, ac_out)))
+    ]
+    for copy in copies:
+        copy.start()
+    for copy in copies:
+        copy.wait()
 
 
 def local(les_state, acoustic_state, mean_flow, projection, target_owner, target_slot):
@@ -661,17 +669,18 @@
         return [vmem(2, n, 8, 128), vmem(2, n, 8, 128), vmem(2, 8, 128)]
 
     field = (8, 8, 128)
-    return pl.pallas_call(
+    shapes = [(5,) + field, (3,) + field, (4,) + field]
+    on_chip = pl.BlockSpec(memory_space=pltpu.VMEM)
+    results = pl.pallas_call(
         functools.partial(kernel, sizes),
         name="coupled_step",
-        out_shape=(
-            jax.ShapeDtypeStruct((5,) + field, F32),
-            jax.ShapeDtypeStruct((3,) + field, F32),
-            jax.ShapeDtypeStruct((4,) + field, F32),
-        ),
-        in_specs=[anywhere, anywhere, anywhere, scalars, scalars, scalars, anywhere],
-        out_specs=(anywhere, anywhere, anywhere),
+        out_shape=tuple(pltpu.VMEM(shape, F32) for shape in shapes),
+        in_specs=[anywhere] * 7,
+        out_specs=(on_chip,) * 3,
         scratch_shapes=[
+            pltpu.SMEM((8, 8), F32),
+            pltpu.SMEM((1, 1, 16), jnp.int32),
+            pltpu.SMEM((1, 1, 16), jnp.int32),
             vmem(5, *field),
             vmem(4, *field),
             vmem(3, *field),
@@ -691,11 +700,7 @@
             *halos(4),
             vmem(5, *field),
             vmem(4, *field),
-            vmem(5, *field),
-            vmem(3, *field),
-            vmem(4, *field),
-            pltpu.SemaphoreType.DMA((4,)),
-            pltpu.SemaphoreType.DMA((3,)),
+            pltpu.SemaphoreType.DMA((7,)),
             pltpu.SemaphoreType.DMA((20,)),
             pltpu.SemaphoreType.DMA((20,)),
             pltpu.SemaphoreType.DMA((4,)),
@@ -703,6 +708,14 @@
         ],
         compiler_params=pltpu.CompilerParams(collective_id=0, has_side_effects=True),
     )(les_state, acoustic_state, mean_flow, projection, target_owner, target_slot, deriv)
+    return pl.pallas_call(
+        write_out,
+        name="write_out",
+        out_shape=tuple(jax.ShapeDtypeStruct(shape, F32) for shape in shapes),
+        in_specs=[on_chip] * 3,
+        out_specs=(anywhere,) * 3,
+        scratch_shapes=[pltpu.SemaphoreType.DMA((3,))],
+    )(*[pltpu.with_memory_space_constraint(result, pltpu.VMEM) for result in results])
 
 
 def solution(mesh):

time: 38.3 us -> 34.4 us (0.90)
  local copies, waits for them, and re-layouts: 3.23 us -> 0 us
  Pallas kernels: 34.2 us -> 33.6 us
    unnamed x7 -> x0, local copies, waits for them, and re-layouts: 3.23 us -> none
    pallas_call x1, Pallas kernels: 34.2 us -> 32.8 us  [local(): pl.pallas_call(functools.partial(kernel, sizes), name='coupled_step', out...]
    pallas_call x0 -> x1, Pallas kernels: none -> 0.77 us  [local(): pl.pallas_call(write_out, name='write_out', out_shape=tuple((jax.ShapeDty...]
where the time goes in v2:
time: 34.4 us; the launch traced here: 34.2 us
  Pallas kernels  33.6 us (98%)
  between operations  0.64 us (2%)
    pallas_call x1, Pallas kernels, local(): pl.pallas_call(functools.partial(kernel, sizes), name='coupled_step', out...  32.8 us
    pallas_call x1, Pallas kernels, local(): pl.pallas_call(write_out, name='write_out', out_shape=tuple((jax.ShapeDty...  0.77 us

profile of v2, /device:TPU:1, one launch (start us, length us, event | category | flops | bytes accessed | tf_op | source)
XLA Modules:
  0.0 34.2 jit_solution(14031034248082365963)
XLA Ops:
  0.6 32.8 %coupled_step.1 = (f32[5,8,8,128]{3,2,1,0:T(8,128)S(1)}, f32[3,8,8,128]{3,2,1,0:T(8,128)S(1)}, f32[4,8,8,128]{3,2,1,0:T(8,128)S(1)}) custom-call(f32[5,8,8,128]{3,2,1,0:T(8,128)} %les.1, f32[4,8,8,128]{3,2,1,0:T(8,128)} %ac.1, f32[3,8,8,128]{3,2,1,0:T(8,128)} %mf.1, f32[8,8]{1,0:T(8,128)} %proj_hbm.1, s32[1,1,16]{2,1,0:T(1,128)} %own_hbm.1, ...), custom_call_target="tpu_custom_call" | custom-call | tf_op jit(solution)/shard_map/coupled_step/pallas_call | solution.py:674
  33.5 0.8 %write_out.1 = (f32[5,8,8,128]{3,2,1,0:T(8,128)}, f32[3,8,8,128]{3,2,1,0:T(8,128)}, f32[4,8,8,128]{3,2,1,0:T(8,128)}) custom-call(f32[5,8,8,128]{3,2,1,0:T(8,128)S(1)} %get-tuple-element.6.les_v, f32[3,8,8,128]{3,2,1,0:T(8,128)S(1)} %get-tuple-element.7.src_v, f32[4,8,8,128]{3,2,1,0:T(8,128)S(1)} %get-tuple-element.8.ac_v), custom_call_target="tpu_custom_call" | custom-call | tf_op jit(solution)/shard_map/write_out/pallas_call | solution.py:711

commit v3 on v2

--- a/solution.py
+++ b/solution.py
@@ -29,7 +29,8 @@
 acoustic_step = 0.01
 upwind_speed = 1.5
 face_lift = 28.0
-REACH = 3
+REACH = 4
+ROWS = 64
 WINDOW = 4
 
 
@@ -227,10 +228,13 @@
 
 
 def pack_faces_z(planes, side):
+    return pack_lane(planes, 127 * side, 0)
+
+
+def pack_lane(planes, at, first):
     face = jnp.zeros((8, 128), F32)
     lane = lanes((8, 128))
-    at = 0 if side == 0 else 127
-    for n, plane in enumerate(planes):
+    for n, plane in enumerate(planes, first):
         face = jnp.where(lane == n, jnp.broadcast_to(plane[:, at : at + 1], (8, 128)), face)
     return face
 
@@ -320,6 +324,11 @@
     mid_halo_x,
     mid_halo_y,
     mid_halo_z,
+    placed_v,
+    side_tiles,
+    side_arrived,
+    end_rows,
+    end_arrived,
     rate_v,
     slope_v,
     load_sem,
@@ -327,6 +336,8 @@
     recv_sem,
     piece_send,
     piece_recv,
+    side_send,
+    side_recv,
 ):
     names = ("gx", "gy", "gz")
     at = [lax.axis_index(name) for name in names]
@@ -383,6 +394,10 @@
         begin = start_of(other)
         return exists(0, distance) & (begin <= me) & (me < begin + WINDOW)
 
+    def grazes(distance):
+        begin = start_of(me + distance)
+        return exists(0, distance) & ((me + 1 == begin) | (me == begin + WINDOW))
+
     for side, distance in ((0, -1), (1, 1)):
         for axis, refs in (
             (0, (halo_x, sec_halo_x, mid_halo_x)),
@@ -398,9 +413,32 @@
     for distance in range(-REACH, REACH + 1):
         if distance != 0:
 
+            grazed, other = (56, 48) if distance > 0 else (48, 56)
+
             @pl.when(jnp.logical_not(comes(distance)))
             def _():
-                arrived[distance + REACH] = jnp.zeros((56, 128), F32)
+                arrived[distance + REACH, 0:48] = jnp.zeros((48, 128), F32)
+                arrived[distance + REACH, other : other + 8] = jnp.zeros((8, 128), F32)
+
+            @pl.when(jnp.logical_not(comes(distance) | grazes(distance)))
+            def _():
+                arrived[distance + REACH, grazed : grazed + 8] = jnp.zeros((8, 128), F32)
+
+    def side_of(n):
+        return 1 + n // 2, 2 * (n % 2) - 1
+
+    def side_comes(n, distance):
+        return exists(*side_of(n)) & comes(distance)
+
+    for n in range(4):
+        for distance in range(-3, 4):
+
+            @pl.when(jnp.logical_not(side_comes(n, distance)))
+            def _():
+                if n < 2:
+                    side_arrived[n, distance + 3] = jnp.zeros((8, 128), F32)
+                else:
+                    end_arrived[n - 2, distance + 3] = jnp.zeros((1, 256), F32)
 
     def message(source, target, axis, side, slot_index):
         distance = -1 if side == 0 else 1
@@ -437,13 +475,16 @@
         (les.at[:, 0 if side == 0 else 7], halo_x.at[1 - side, 0:5], 0, side, side)
         for side in range(2)
     ]
-    sound_x = [
+    flow_y = [
+        (send_y.at[side, 0:5], halo_y.at[1 - side, 0:5], 1, side, 4 + side) for side in range(2)
+    ]
+    both_z = [(send_z.at[side], halo_z.at[1 - side], 2, side, 6 + side) for side in range(2)]
+    sound = [
         (ac.at[:, 0 if side == 0 else 7], halo_x.at[1 - side, 5:9], 0, side, 2 + side)
         for side in range(2)
+    ] + [
+        (send_y.at[side, 5:9], halo_y.at[1 - side, 5:9], 1, side, 20 + side) for side in range(2)
     ]
-    near_yz = [
-        (send_y.at[side], halo_y.at[1 - side], 1, side, 4 + side) for side in range(2)
-    ] + [(send_z.at[side], halo_z.at[1 - side], 2, side, 6 + side) for side in range(2)]
     section = (
         [
             (sec_v.at[:, 0 if side == 0 else 7], sec_halo_x.at[1 - side], 0, side, 8 + side)
@@ -487,8 +528,9 @@
             side,
         )
 
-    begin(near_yz)
-    begin(sound_x)
+    begin(flow_y)
+    begin(both_z)
+    begin(sound)
     for load in loads[2:]:
         load.wait()
 
@@ -504,12 +546,10 @@
         ],
         axis=0,
     )
-    for w in range(WINDOW):
-        pieces[w, 48:56] = quarter_transpose([labels] * 4, w)
-
     state = [les_v[c] for c in range(5)]
     halo = Halo(halo_x, halo_y, halo_z, 0)
-    arrive(near_yz)
+    arrive(flow_y)
+    arrive(both_z)
     arrive(flow_x)
     lamb = lamb_vector(state, halo)
     cells = jnp.concatenate([part.reshape(64, 128) for part in lamb], axis=1)
@@ -521,28 +561,108 @@
     both = dot_nt(jnp.concatenate([plane_high, plane_low], axis=1), column_operand)
     placed = both[:, :128] + both[:, 128:]
     groups = [placed[48 * g : 48 * g + 48] for g in range(4)]
+    lows = [placed[64 * c : 64 * c + 8] for c in range(3)] + [labels]
+    highs = [placed[64 * c + 56 : 64 * c + 64] for c in range(3)] + [labels]
     for w in range(WINDOW):
-        pieces[w, 0:48] = quarter_transpose(groups, w)
+        pieces[w + 1, 0:48] = quarter_transpose(groups, w)
+    lane = lanes((8, 128))
+    row = rows((8, 128))
+    for w in range(-1, WINDOW + 1):
+        zero = jnp.zeros((8, 128), F32)
+        above = quarter_transpose(highs, w - 1) if w >= 1 else zero
+        below = quarter_transpose(lows, w + 1) if w + 1 < WINDOW else zero
+        if 0 <= w < WINDOW:
+            moved = labels if w == 3 else pltpu.roll(labels, 32 * (3 - w), 1)
+            above = jnp.where((lane >= 96) & (row >= 4), moved, above)
+        pieces[w + 1, 48:56] = above
+        pieces[w + 1, 56:64] = below
 
     def piece_copy(w):
         target = start + w
         slot_index = me - target + REACH
         return pltpu.make_async_remote_copy(
-            src_ref=pieces.at[w],
+            src_ref=pieces.at[w + 1],
             dst_ref=arrived.at[slot_index],
-            send_sem=piece_send.at[w],
+            send_sem=piece_send.at[w + 1],
             recv_sem=piece_recv.at[slot_index],
             device_id={"gx": target},
             device_id_type=MESH,
         )
 
+    def edge_copy(w):
+        target = start + w
+        slot_index = me - target + REACH
+        part = slice(56, 64) if w < 0 else slice(48, 56)
+        return pltpu.make_async_remote_copy(
+            src_ref=pieces.at[w + 1, part],
+            dst_ref=arrived.at[slot_index, part],
+            send_sem=piece_send.at[w + 1],
+            recv_sem=piece_recv.at[slot_index],
+            device_id={"gx": target},
+            device_id_type=MESH,
+        )
+
     for w in range(WINDOW):
 
         @pl.when(start + w != me)
         def _():
             piece_copy(w).start()
 
-    arrived[REACH] = pieces[me - start]
+    @pl.when(start >= 1)
+    def _():
+        edge_copy(-1).start()
+
+    @pl.when(start + WINDOW < count_x)
+    def _():
+        edge_copy(WINDOW).start()
+
+    arrived[REACH] = pieces[me - start + 1]
+
+    def side_copy(n, w):
+        axis, distance = side_of(n)
+        target = start + w
+        slot_index = me - target + 3
+        landing = n + 1 - 2 * (n % 2)
+        if n < 2:
+            source, goal = side_tiles.at[n, w], side_arrived.at[landing, slot_index]
+        else:
+            source, goal = end_rows.at[4 * (n - 2) + w], end_arrived.at[landing - 2, slot_index]
+        return pltpu.make_async_remote_copy(
+            src_ref=source,
+            dst_ref=goal,
+            send_sem=side_send.at[4 * n + w],
+            recv_sem=side_recv.at[7 * landing + slot_index],
+            device_id={"gx": target, names[axis]: at[axis] + distance},
+            device_id_type=MESH,
+        )
+
+    def side_begin(n):
+        @pl.when(exists(*side_of(n)))
+        def _():
+            for w in range(WINDOW):
+                side_copy(n, w).start()
+
+    placed_v[...] = placed.reshape(3, 8, 8, 128)
+    for n in range(2):
+        parts = [placed_v[c, :, 7 * n, :] for c in range(3)] + [labels]
+        for w in range(WINDOW):
+            side_tiles[n, w] = quarter_transpose(parts, w)
+        side_begin(n)
+    upper = row >= 4
+    wanted = (
+        (lane // 32 == row % 4)
+        & (lane % 8 == jnp.where(upper, 7, 0))
+        & (labels == jnp.where(upper, 15.0, 0.0))
+    )
+    ends = jnp.where(wanted, 1.0, 0.0).astype(BF16)
+    placed_high, placed_low = split(
+        jnp.concatenate([placed, jnp.zeros((64, 128), F32)], axis=0)
+    )
+    sums = dot_nt(ends, placed_high) + dot_nt(ends, placed_low)
+    for n in range(8):
+        end_rows[n] = sums[n : n + 1]
+    side_begin(2)
+    side_begin(3)
 
     rate = les_rate(state, halo)
     for c in range(5):
@@ -556,11 +676,17 @@
     begin(section)
 
     mean_speed = [mf_v[c] for c in range(3)]
-    arrive(sound_x)
-    sound = [ac_v[c] for c in range(4)]
-    slopes = acoustic_rate(sound, mean_speed, Halo(halo_x, halo_y, halo_z, 5), deriv_v)
+    arrive(sound)
+    slopes = acoustic_rate(
+        [ac_v[c] for c in range(4)], mean_speed, Halo(halo_x, halo_y, halo_z, 5), deriv_v
+    )
     for c in range(4):
         slope_v[c] = slopes[c]
+        mid_v[c] = ac_v[c] + acoustic_step * slopes[c]
+    for side in range(2):
+        mid_send_y[side] = mid_v[:, :, 0 if side == 0 else 7, :]
+        mid_send_z[side] = pack_faces_z([mid_v[c, x] for c in range(4) for x in range(8)], side)
+    begin(middle)
 
     for distance in range(-REACH, REACH + 1):
         if distance != 0:
@@ -576,44 +702,96 @@
                     device_id_type=MESH,
                 ).wait_recv()
 
-    halves = []
-    tags = []
-    zero = jnp.zeros((48, 128), F32)
+            @pl.when(grazes(distance))
+            def _():
+                part = slice(56, 64) if distance > 0 else slice(48, 56)
+                pltpu.make_async_remote_copy(
+                    src_ref=pieces.at[0, part],
+                    dst_ref=arrived.at[distance + REACH, part],
+                    send_sem=piece_send.at[0],
+                    recv_sem=piece_recv.at[distance + REACH],
+                    device_id={"gx": me + distance},
+                    device_id_type=MESH,
+                ).wait_recv()
+
+    for n in range(4):
+        for distance in range(-3, 4):
+
+            @pl.when(side_comes(n, distance))
+            def _():
+                axis, step = side_of(n)
+                if n < 2:
+                    source, goal = side_tiles.at[0, 0], side_arrived.at[n, distance + 3]
+                else:
+                    source, goal = end_rows.at[0], end_arrived.at[n - 2, distance + 3]
+                pltpu.make_async_remote_copy(
+                    src_ref=source,
+                    dst_ref=goal,
+                    send_sem=side_send.at[0],
+                    recv_sem=side_recv.at[7 * n + distance + 3],
+                    device_id={"gx": me + distance, names[axis]: at[axis] + step},
+                    device_id_type=MESH,
+                ).wait_recv()
+
+    same = (lanes((8, 128)) % 8) == rows((8, 128))
+
+    def picks_of(tags):
+        return jnp.concatenate(
+            [
+                jnp.concatenate(
+                    [jnp.where((tag == float(n)) & same, 1.0, 0.0) for n in range(16)], axis=0
+                )
+                for tag in tags
+            ],
+            axis=1,
+        ).astype(BF16)
+
+    def gather(halves, tags):
+        picks = picks_of(tags)
+        high, low = split(jnp.concatenate(halves, axis=1))
+        return dot_nt(high, picks) + dot_nt(low, picks)
+
+    def members_of(half, first, part):
+        members = [first + REACH + 4 * half + n for n in range(4)]
+        zero = jnp.zeros((part.stop - part.start, 128), F32)
+        return [arrived[n, part] if 4 * half + k < 7 else zero for k, n in enumerate(members)]
+
+    halves, tags = [], []
     for half in range(2):
-        members = [4 * half + n for n in range(4)]
-        parts = [arrived[n, 0:48] if n < 7 else zero for n in members]
-        quarter = [quarter_transpose(parts, g) for g in range(4)]
-        halves.append(jnp.concatenate(quarter, axis=0))
-        tag = jnp.zeros((8, 128), F32)
-        for n in members:
-            if n < 7:
-                tag = jnp.where(lanes((8, 128)) // 32 == n % 4, arrived[n, 48:56], tag)
-        tags.append(tag)
-    same = (lanes((8, 128)) % 8) == rows((8, 128))
-    picks = jnp.concatenate(
-        [
-            jnp.concatenate(
-                [jnp.where((tag == float(s)) & same, 1.0, 0.0) for s in range(16)], axis=0
+        parts = members_of(half, -3, slice(0, 48))
+        halves.append(
+            jnp.concatenate([quarter_transpose(parts, g) for g in range(4)], axis=0)
+        )
+        tag = quarter_transpose(members_of(half, -3, slice(48, 56)), 3)
+        tags.append(jnp.broadcast_to(tag[4:5], (8, 128)))
+    src_v[...] = gather(halves, tags).reshape(3, 8, 8, 128)
+
+    def gather_tiles(tiles):
+        halves, tags = [], []
+        for parts in (tiles[:4], tiles[4:] + [jnp.zeros((8, 128), F32)]):
+            halves.append(
+                jnp.concatenate([quarter_transpose(parts, c) for c in range(3)], axis=0)
             )
-            for tag in tags
-        ],
-        axis=1,
-    ).astype(BF16)
-    gathered = jnp.concatenate(halves, axis=1)
-    gathered_high, gathered_low = split(gathered)
-    source = dot_nt(gathered_high, picks) + dot_nt(gathered_low, picks)
-    source = source.reshape(3, 8, 8, 128)
-    src_v[...] = source
-    for c in range(4):
-        if c > 0:
-            slope_v[c] = slope_v[c] + src_v[c - 1]
-        mid_v[c] = ac_v[c] + acoustic_step * slope_v[c]
+            tag = quarter_transpose(parts, 3)
+            tags.append(jnp.broadcast_to(tag[0:1], (8, 128)))
+        return gather(halves, tags)
+
+    source_x = [
+        gather_tiles([arrived[first + n, part] for n in range(7)])
+        for first, part in ((0, slice(48, 56)), (2, slice(56, 64)))
+    ]
+    line = lax.broadcasted_iota(jnp.int32, (256, 128), 0)
+    folds = jnp.where(lanes((256, 128)) == 8 + line // 8, 1.0, 0.0).astype(BF16)
+    source_z = []
     for side in range(2):
-        mid_send_y[side] = mid_v[:, :, 0 if side == 0 else 7, :]
-        mid_send_z[side] = pack_faces_z(
-            [mid_v[c, x] for c in range(4) for x in range(8)], side
-        )
-    begin(middle)
+        line_sum = end_arrived[side, 0]
+        for n in range(1, 7):
+            line_sum = line_sum + end_arrived[side, n]
+        spread = jnp.broadcast_to(line_sum, (8, 256))
+        spread = jnp.where(lanes((8, 256)) % 8 == rows((8, 256)), spread, 0.0)
+        spread_high, spread_low = split(spread)
+        source_z.append(dot_nn(spread_high, folds) + dot_nn(spread_low, folds))
+    source_y = [gather_tiles([side_arrived[side, n] for n in range(7)]) for side in range(2)]
 
     arrive(section)
     rate = les_rate([sec_v[c] for c in range(5)], Halo(sec_halo_x, sec_halo_y, sec_halo_z, 0))
@@ -621,23 +799,45 @@
         les_next[c] = les_v[c] + 0.5 * (rate_v[c] + rate[c])
 
     arrive(middle)
+    for side in range(2):
+        mid_halo_z[side] = mid_halo_z[side] + acoustic_step * source_z[side]
+        for c in range(3):
+            for ref, face in ((mid_halo_x, source_x[side]), (mid_halo_y, source_y[side])):
+                ref[side, 1 + c] = ref[side, 1 + c] + acoustic_step * face[8 * c : 8 * c + 8]
     slopes = acoustic_rate(
-        [mid_v[c] for c in range(4)],
-        [mf_v[c] for c in range(3)],
+        [mid_v[0]] + [mid_v[1 + c] + acoustic_step * src_v[c] for c in range(3)],
+        mean_speed,
         Halo(mid_halo_x, mid_halo_y, mid_halo_z, 0),
         deriv_v,
     )
     for c in range(4):
         total = slope_v[c] + slopes[c]
         if c > 0:
-            total = total + src_v[c - 1]
+            total = total + 2.0 * src_v[c - 1]
         ac_next[c] = ac_v[c] + 0.5 * acoustic_step * total
 
     drain(flow_x)
-    drain(sound_x)
-    drain(near_yz)
+    drain(flow_y)
+    drain(both_z)
+    drain(sound)
     drain(section)
     drain(middle)
+
+    for n in range(4):
+
+        @pl.when(exists(*side_of(n)))
+        def _():
+            for w in range(WINDOW):
+                side_copy(n, w).wait_send()
+
+    @pl.when(start >= 1)
+    def _():
+        edge_copy(-1).wait_send()
+
+    @pl.when(start + WINDOW < count_x)
+    def _():
+        edge_copy(WINDOW).wait_send()
+
     for w in range(WINDOW):
 
         @pl.when(start + w != me)
@@ -688,8 +888,8 @@
             vmem(2, 9, 8, 128),
             vmem(2, 8, 128),
             *halos(9),
-            vmem(4, 56, 128),
-            vmem(7, 56, 128),
+            vmem(6, ROWS, 128),
+            vmem(9, ROWS, 128),
             vmem(5, *field),
             vmem(2, 5, 8, 128),
             vmem(2, 8, 128),
@@ -698,13 +898,20 @@
             vmem(2, 4, 8, 128),
             vmem(2, 8, 128),
             *halos(4),
+            vmem(3, *field),
+            vmem(2, 4, 8, 128),
+            vmem(2, 7, 8, 128),
+            vmem(8, 1, 256),
+            vmem(2, 7, 1, 256),
             vmem(5, *field),
             vmem(4, *field),
             pltpu.SemaphoreType.DMA((7,)),
-            pltpu.SemaphoreType.DMA((20,)),
-            pltpu.SemaphoreType.DMA((20,)),
-            pltpu.SemaphoreType.DMA((4,)),
-            pltpu.SemaphoreType.DMA((7,)),
+            pltpu.SemaphoreType.DMA((22,)),
+            pltpu.SemaphoreType.DMA((22,)),
+            pltpu.SemaphoreType.DMA((6,)),
+            pltpu.SemaphoreType.DMA((9,)),
+            pltpu.SemaphoreType.DMA((16,)),
+            pltpu.SemaphoreType.DMA((28,)),
         ],
         compiler_params=pltpu.CompilerParams(collective_id=0, has_side_effects=True),
     )(les_state, acoustic_state, mean_flow, projection, target_owner, target_slot, deriv)

time: 34.4 us -> 32.2 us (0.936)
  Pallas kernels: 33.6 us -> 31.2 us
    pallas_call x1, Pallas kernels: 32.8 us -> 30.4 us  [local(): pl.pallas_call(functools.partial(kernel, sizes), name='coupled_step', out...]
where the time goes in v3:
time: 32.2 us; the launch traced here: 31.8 us
  Pallas kernels  31.2 us (97%)
  between operations  0.64 us (2%)
    pallas_call x1, Pallas kernels, local(): pl.pallas_call(functools.partial(kernel, sizes), name='coupled_step', out...  30.4 us
    pallas_call x1, Pallas kernels, local(): pl.pallas_call(write_out, name='write_out', out_shape=tuple((jax.ShapeDty...  0.77 us

profile of v3, /device:TPU:1, one launch (start us, length us, event | category | flops | bytes accessed | tf_op | source)
XLA Modules:
  0.0 31.8 jit_solution(17749977087574947349)
XLA Ops:
  0.6 30.4 %coupled_step.1 = (f32[5,8,8,128]{3,2,1,0:T(8,128)S(1)}, f32[3,8,8,128]{3,2,1,0:T(8,128)S(1)}, f32[4,8,8,128]{3,2,1,0:T(8,128)S(1)}) custom-call(f32[5,8,8,128]{3,2,1,0:T(8,128)} %les.1, f32[4,8,8,128]{3,2,1,0:T(8,128)} %ac.1, f32[3,8,8,128]{3,2,1,0:T(8,128)} %mf.1, f32[8,8]{1,0:T(8,128)} %proj_hbm.1, s32[1,1,16]{2,1,0:T(1,128)} %own_hbm.1, ...), custom_call_target="tpu_custom_call" | custom-call | tf_op jit(solution)/shard_map/coupled_step/pallas_call | solution.py:874
  31.0 0.8 %write_out.1 = (f32[5,8,8,128]{3,2,1,0:T(8,128)}, f32[3,8,8,128]{3,2,1,0:T(8,128)}, f32[4,8,8,128]{3,2,1,0:T(8,128)}) custom-call(f32[5,8,8,128]{3,2,1,0:T(8,128)S(1)} %get-tuple-element.6.les_v, f32[3,8,8,128]{3,2,1,0:T(8,128)S(1)} %get-tuple-element.7.src_v, f32[4,8,8,128]{3,2,1,0:T(8,128)S(1)} %get-tuple-element.8.ac_v), custom_call_target="tpu_custom_call" | custom-call | tf_op jit(solution)/shard_map/write_out/pallas_call | solution.py:918

commit v4 on v3

--- a/solution.py
+++ b/solution.py
@@ -30,6 +30,7 @@
 upwind_speed = 1.5
 face_lift = 28.0
 REACH = 4
+GREET = 4
 ROWS = 64
 WINDOW = 4
 
@@ -350,8 +351,8 @@
 
     barrier = pltpu.get_barrier_semaphore()
     expected = jnp.int32(0)
-    for axis, reach in ((0, REACH), (1, 1), (2, 1)):
-        for distance in range(-reach, reach + 1):
+    for axis, reach in ((0, GREET), (1, 1), (2, 1)):
+        for distance in sorted(range(-reach, reach + 1), key=abs):
             if distance == 0:
                 continue
             near = exists(axis, distance)
@@ -472,7 +473,7 @@
                 message(source, target, axis, side, slot_index).wait_send()
 
     flow_x = [
-        (les.at[:, 0 if side == 0 else 7], halo_x.at[1 - side, 0:5], 0, side, side)
+        (les_v.at[:, 0 if side == 0 else 7], halo_x.at[1 - side, 0:5], 0, side, side)
         for side in range(2)
     ]
     flow_y = [
@@ -480,7 +481,7 @@
     ]
     both_z = [(send_z.at[side], halo_z.at[1 - side], 2, side, 6 + side) for side in range(2)]
     sound = [
-        (ac.at[:, 0 if side == 0 else 7], halo_x.at[1 - side, 5:9], 0, side, 2 + side)
+        (ac_v.at[:, 0 if side == 0 else 7], halo_x.at[1 - side, 5:9], 0, side, 2 + side)
         for side in range(2)
     ] + [
         (send_y.at[side, 5:9], halo_y.at[1 - side, 5:9], 1, side, 20 + side) for side in range(2)
@@ -514,8 +515,6 @@
         ]
     )
 
-    pl.semaphore_wait(barrier, expected)
-    begin(flow_x)
     for load in loads[:2]:
         load.wait()
     for side in range(2):
@@ -528,6 +527,8 @@
             side,
         )
 
+    pl.semaphore_wait(barrier, expected)
+    begin(flow_x)
     begin(flow_y)
     begin(both_z)
     begin(sound)
@@ -602,19 +603,19 @@
             device_id_type=MESH,
         )
 
+    @pl.when(start >= 1)
+    def _():
+        edge_copy(-1).start()
+
+    @pl.when(start + WINDOW < count_x)
+    def _():
+        edge_copy(WINDOW).start()
+
     for w in range(WINDOW):
 
         @pl.when(start + w != me)
         def _():
             piece_copy(w).start()
-
-    @pl.when(start >= 1)
-    def _():
-        edge_copy(-1).start()
-
-    @pl.when(start + WINDOW < count_x)
-    def _():
-        edge_copy(WINDOW).start()
 
     arrived[REACH] = pieces[me - start + 1]
 
@@ -687,6 +688,10 @@
         mid_send_y[side] = mid_v[:, :, 0 if side == 0 else 7, :]
         mid_send_z[side] = pack_faces_z([mid_v[c, x] for c in range(4) for x in range(8)], side)
     begin(middle)
+    drain(flow_x)
+    drain(flow_y)
+    drain(both_z)
+    drain(sound)
 
     for distance in range(-REACH, REACH + 1):
         if distance != 0:
@@ -714,6 +719,38 @@
                     device_id_type=MESH,
                 ).wait_recv()
 
+    same = (lanes((8, 128)) % 8) == rows((8, 128))
+
+    def picks_of(tags):
+        return jnp.concatenate(
+            [
+                jnp.concatenate(
+                    [jnp.where((tag == float(n)) & same, 1.0, 0.0) for n in range(16)], axis=0
+                )
+                for tag in tags
+            ],
+            axis=1,
+        ).astype(BF16)
+
+    def gather(halves, tags):
+        picks = picks_of(tags)
+        high, low = split(jnp.concatenate(halves, axis=1))
+        return dot_nt(high, picks) + dot_nt(low, picks)
+
+    def members_of(half, first, part):
+        members = [first + REACH + 4 * half + n for n in range(4)]
+        zero = jnp.zeros((part.stop - part.start, 128), F32)
+        return [arrived[n, part] if 4 * half + k < 7 else zero for k, n in enumerate(members)]
+
+    halves, tags = [], []
+    for half in range(2):
+        parts = members_of(half, -3, slice(0, 48))
+        halves.append(
+            jnp.concatenate([quarter_transpose(parts, g) for g in range(4)], axis=0)
+        )
+        tag = quarter_transpose(members_of(half, -3, slice(48, 56)), 3)
+        tags.append(jnp.broadcast_to(tag[4:5], (8, 128)))
+    src_v[...] = gather(halves, tags).reshape(3, 8, 8, 128)
     for n in range(4):
         for distance in range(-3, 4):
 
@@ -733,38 +770,6 @@
                     device_id_type=MESH,
                 ).wait_recv()
 
-    same = (lanes((8, 128)) % 8) == rows((8, 128))
-
-    def picks_of(tags):
-        return jnp.concatenate(
-            [
-                jnp.concatenate(
-                    [jnp.where((tag == float(n)) & same, 1.0, 0.0) for n in range(16)], axis=0
-                )
-                for tag in tags
-            ],
-            axis=1,
-        ).astype(BF16)
-
-    def gather(halves, tags):
-        picks = picks_of(tags)
-        high, low = split(jnp.concatenate(halves, axis=1))
-        return dot_nt(high, picks) + dot_nt(low, picks)
-
-    def members_of(half, first, part):
-        members = [first + REACH + 4 * half + n for n in range(4)]
-        zero = jnp.zeros((part.stop - part.start, 128), F32)
-        return [arrived[n, part] if 4 * half + k < 7 else zero for k, n in enumerate(members)]
-
-    halves, tags = [], []
-    for half in range(2):
-        parts = members_of(half, -3, slice(0, 48))
-        halves.append(
-            jnp.concatenate([quarter_transpose(parts, g) for g in range(4)], axis=0)
-        )
-        tag = quarter_transpose(members_of(half, -3, slice(48, 56)), 3)
-        tags.append(jnp.broadcast_to(tag[4:5], (8, 128)))
-    src_v[...] = gather(halves, tags).reshape(3, 8, 8, 128)
 
     def gather_tiles(tiles):
         halves, tags = [], []
@@ -816,10 +821,6 @@
             total = total + 2.0 * src_v[c - 1]
         ac_next[c] = ac_v[c] + 0.5 * acoustic_step * total
 
-    drain(flow_x)
-    drain(flow_y)
-    drain(both_z)
-    drain(sound)
     drain(section)
     drain(middle)
 

time: 32.2 us -> 32 us (level)
  no operation moved by 1% of the time
where the time goes in v4:
time: 32 us; the launch traced here: 31.6 us
  Pallas kernels  31 us (97%)
  between operations  0.64 us (2%)
    pallas_call x1, Pallas kernels, local(): pl.pallas_call(functools.partial(kernel, sizes), name='coupled_step', out...  30.2 us
    pallas_call x1, Pallas kernels, local(): pl.pallas_call(write_out, name='write_out', out_shape=tuple((jax.ShapeDty...  0.77 us

profile of v4, /device:TPU:1, one launch (start us, length us, event | category | flops | bytes accessed | tf_op | source)
XLA Modules:
  0.0 31.6 jit_solution(2687119951534996933)
XLA Ops:
  0.6 30.2 %coupled_step.1 = (f32[5,8,8,128]{3,2,1,0:T(8,128)S(1)}, f32[3,8,8,128]{3,2,1,0:T(8,128)S(1)}, f32[4,8,8,128]{3,2,1,0:T(8,128)S(1)}) custom-call(f32[5,8,8,128]{3,2,1,0:T(8,128)} %les.1, f32[4,8,8,128]{3,2,1,0:T(8,128)} %ac.1, f32[3,8,8,128]{3,2,1,0:T(8,128)} %mf.1, f32[8,8]{1,0:T(8,128)} %proj_hbm.1, s32[1,1,16]{2,1,0:T(1,128)} %own_hbm.1, ...), custom_call_target="tpu_custom_call" | custom-call | tf_op jit(solution)/shard_map/coupled_step/pallas_call | solution.py:875
  30.8 0.8 %write_out.1 = (f32[5,8,8,128]{3,2,1,0:T(8,128)}, f32[3,8,8,128]{3,2,1,0:T(8,128)}, f32[4,8,8,128]{3,2,1,0:T(8,128)}) custom-call(f32[5,8,8,128]{3,2,1,0:T(8,128)S(1)} %get-tuple-element.6.les_v, f32[3,8,8,128]{3,2,1,0:T(8,128)S(1)} %get-tuple-element.7.src_v, f32[4,8,8,128]{3,2,1,0:T(8,128)S(1)} %get-tuple-element.8.ac_v), custom_call_target="tpu_custom_call" | custom-call | tf_op jit(solution)/shard_map/write_out/pallas_call | solution.py:919
